TPU v7x, 256 devices: a whole 4x4x8 slice. The times are simulated.
256 devices in a mesh: rad: 8 (over z_hi, core), azi: 32 (over y, z_lo, x).
Axes of the slice: x: 4, y: 4, z: 8 (z_hi: 4, z_lo: 2; z = z_hi * 2 + z_lo), core: 2. Of those that a mesh axis runs over, the one named last changes fastest.
Arguments:
- density: float32 [4, 256, 16384], P(None, 'rad', 'azi'), may hold values from -6 to 6
- radial_velocity: float32 [4, 256, 16384], P(None, 'rad', 'azi'), may hold values from -6 to 6
- azimuthal_velocity: float32 [4, 256, 16384], P(None, 'rad', 'azi'), may hold values from -6 to 6
- cycle_shift: int32 [256], P('rad'), may hold values from 0 to 16383
- remainder: float32 [256], P('rad'), may hold values from 0 to 1
- kernel: bfloat16 [2048, 256, 256], P(('rad', 'azi')), may hold values from -0.375 to 0.375
Outputs:
- density_next: float32 [4, 256, 16384], P(None, 'rad', 'azi')
- radial_next: float32 [4, 256, 16384], P(None, 'rad', 'azi')
- azimuthal_next: float32 [4, 256, 16384], P(None, 'rad', 'azi')
- potential: float32 [256, 16384], P(('rad', 'azi'))
All inputs are finite; a program needn't handle non-finite values.
Results may differ from a plain program's by a relative error of at most 0.0003.
The roundings to bfloat16 on the way count: a program that leaves them out, or rounds other values in their place, can miss the bound.
Values may be sent and summed in bfloat16 or wider, within the bound.
A program may use at most 256 MiB of HBM per device.

v0:
```python
import numpy as np

import jax
import jax.numpy as jnp
from jax import lax
from jax.experimental import pallas as pl
from jax.experimental.pallas import tpu as pltpu
from jax.sharding import PartitionSpec as P

NZ = 4
NPHI = 16384
MODES = 2048
NR = 256
RAD = 8
AZI = 32
SLAB = NR // RAD
SEG = NPHI // AZI
LANES = 128
QUADS = SEG // LANES
MEMBERS = 3 * NZ
ROWS = MEMBERS * QUADS
EXT_R = SLAB + 8
EXT_P = SEG + LANES
RADIAL_COURANT = 0.3
VISCOSITY = 0.08
HIGHEST = lax.Precision.HIGHEST
F32 = jnp.float32
MESH = pl.DeviceIdType.MESH


def tables():
    n = np.arange(128)
    turn = 2.0 * np.pi / 128 * (np.outer(n, n) % 128)
    first = np.concatenate([np.cos(turn), -np.sin(turn)], axis=0)
    last = np.concatenate([np.cos(turn), -np.sin(turn)], axis=1)
    small = 2.0 * np.pi / NPHI * np.outer(n, n)
    twiddle = np.concatenate([np.cos(small), np.sin(small)], axis=0)
    col = np.arange(256)
    half, ring, part = col // 128, col % 16 // 2, col % 2
    phi = 2.0 * np.pi / 128 * (np.outer(n, 2 * ring + half) % 128)
    cos, sin = np.cos(phi), np.sin(phi)
    real = part == 0
    straight = np.concatenate([np.where(real, cos, -sin), np.where(real, sin, cos)], axis=0)
    turned = np.concatenate([np.where(real, sin, cos), np.where(real, -cos, sin)], axis=0)
    real = real[:, None]
    back = np.concatenate(
        [np.where(real, cos.T, -sin.T), np.where(real, sin.T, cos.T)], axis=1
    )
    return [t.astype(np.float32) for t in (first, last, twiddle, straight, turned, back)]


def dot(left, right):
    return jnp.dot(left, right, precision=HIGHEST, preferred_element_type=F32)


def iota(shape, axis):
    return lax.broadcasted_iota(jnp.int32, shape, axis)


def wide(value, count):
    return jnp.concatenate([value] * count, axis=1)


def cubic_weights(remainder):
    moved = -remainder
    w_next = moved * (moved + 1.0) * (moved + 2.0) / 6.0
    w_here = -(moved - 1.0) * (moved + 1.0) * (moved + 2.0) / 2.0
    w_prev = (moved - 1.0) * moved * (moved + 2.0) / 2.0
    w_prev_two = -(moved - 1.0) * moved * (moved + 1.0) / 6.0
    return w_next, w_here, w_prev, w_prev_two


def rates(get, z, rows, coeffs):
    courant, coriolis, epicycle = coeffs
    below, above = max(z - 1, 0), min(z + 1, NZ - 1)
    center, ahead, rad_diff, azi_diff, spread = [], [], [], [], []
    for c in range(3):
        whole = get(c, z)
        inner = pltpu.roll(whole, 1, 0)[:rows]
        outer = pltpu.roll(whole, EXT_R - 1, 0)[:rows]
        mid = whole[:rows]
        prev = pltpu.roll(mid, 1, 1)
        following = pltpu.roll(mid, EXT_P - 1, 1)
        center.append(mid)
        rad_diff.append(outer - inner if c < 2 else None)
        azi_diff.append(following - prev if c != 1 else None)
        total = (get(c, below)[:rows] + get(c, above)[:rows]) + (inner + outer) + (prev + following)
        spread.append(VISCOSITY * (total - 6.0 * mid))
    half = 0.5 * RADIAL_COURANT
    change = (
        spread[0] - (half * rad_diff[1] + courant * azi_diff[2]),
        spread[1] + coriolis * center[2] - half * rad_diff[0],
        spread[2] - epicycle * center[1] - courant * azi_diff[0],
    )
    return change, center


def body(
    density, radial_velocity, azimuthal_velocity, shift, rest, kernel, first, last, twiddle, straight,
    turned, back, density_out, radial_out, azimuthal_out, potential,
    ext, sect, coef, weight, row_send, row_in, tile_in, col_send, col_in, move_out, cycle_in, cycle_out,
    move_in, total, surf_out, surf_in, spec_out, spec_in, modes_out, modes_in, pot_out, pot_in, back_out,
    back_in, kern, t_first, t_last, t_twiddle, t_straight, t_turned, t_back,
    local_sem, halo_send, halo_recv, send_sem, recv_sem,
):
    rad, azi = lax.axis_index("rad"), lax.axis_index("azi")
    outer, inner = lax.rem(rad + 1, RAD), lax.rem(rad + RAD - 1, RAD)
    right, left = lax.rem(azi + 1, AZI), lax.rem(azi + AZI - 1, AZI)

    loads = [
        pltpu.make_async_copy(src, ext.at[pl.ds(NZ * c, NZ), pl.ds(0, SLAB), pl.ds(0, SEG)], local_sem.at[c])
        for c, src in enumerate((density, radial_velocity, azimuthal_velocity))
    ]
    for n, (src, dst) in enumerate(
        (
            (first, t_first), (twiddle, t_twiddle), (straight, t_straight), (turned, t_turned),
            (kernel, kern), (back, t_back), (last, t_last),
        )
    ):
        loads.append(pltpu.make_async_copy(src, dst, local_sem.at[3 + n]))
    for load in loads:
        load.start()

    col_in[...] = jnp.zeros(col_in.shape, F32)
    barrier = pltpu.get_barrier_semaphore()

    def greet_azi(step, carry):
        pl.semaphore_signal(
            barrier, inc=1, device_id={"rad": rad, "azi": lax.rem(azi + step, AZI)}, device_id_type=MESH
        )
        return carry

    def greet_rad(step, carry):
        pl.semaphore_signal(
            barrier, inc=1, device_id={"rad": lax.rem(rad + step, RAD), "azi": azi}, device_id_type=MESH
        )
        return carry

    for r_to in (outer, inner):
        for a_to in (right, left):
            pl.semaphore_signal(barrier, inc=1, device_id={"rad": r_to, "azi": a_to}, device_id_type=MESH)
    lax.fori_loop(1, AZI, greet_azi, 0)
    lax.fori_loop(1, RAD, greet_rad, 0)

    row = iota((EXT_R, LANES), 0)
    cycle = SLAB * rad + jnp.where(row < SLAB + 4, row, row - EXT_R)
    radius = 1.0 + 4.0 * (cycle.astype(F32) + 0.5) / NR
    steep = 1.0 / (radius * jnp.sqrt(radius))
    coef[0] = 0.15 / radius
    coef[1] = 0.2 * steep
    coef[2] = 0.05 * steep
    block_row = iota((8, LANES), 0)
    for block in range(SLAB // 8):
        fraction = jnp.zeros((8, LANES), F32)
        for n in range(8):
            fraction = jnp.where(block_row == n, rest[8 * block + n], fraction)
        for n, value in enumerate(cubic_weights(fraction)):
            weight[n, pl.ds(8 * block, 8), :] = value
    ext[:, pl.ds(SLAB, 8), :] = jnp.zeros((MEMBERS, 8, EXT_P), F32)

    for load in loads[:3]:
        load.wait()
    lane_tile = iota((SLAB, LANES), 1)
    mixed = []
    for m in range(MEMBERS):
        low = ext[m, pl.ds(0, SLAB), pl.ds(0, LANES)]
        high = ext[m, pl.ds(0, SLAB), pl.ds(SEG - LANES, LANES)]
        edge = jnp.where(lane_tile < LANES // 2, low, high)
        mixed.append(edge)
        for n, at in enumerate((SLAB - 2, 0)):
            row_send[n, pl.ds(2 * m, 2), pl.ds(0, SEG)] = ext[m, pl.ds(at, 2), pl.ds(0, SEG)]
            row_send[n, pl.ds(2 * m, 2), pl.ds(SEG, LANES)] = edge[at : at + 2]
    columns = jnp.concatenate(mixed, axis=0).T
    col_send[0] = columns[LANES - 8 :]
    col_send[1] = columns[:8]

    pl.semaphore_wait(barrier, AZI - 1 + RAD - 1 + 4)

    def halo(n, src, dst, r_to, a_to):
        return pltpu.make_async_remote_copy(
            src_ref=src, dst_ref=dst, send_sem=halo_send.at[n], recv_sem=halo_recv.at[n],
            device_id={"rad": r_to, "azi": a_to}, device_id_type=MESH,
        )

    plain, corner = pl.ds(0, SEG), pl.ds(SEG, LANES)
    halos = [
        halo(0, row_send.at[0, :, plain], row_in.at[0], outer, azi),
        halo(1, row_send.at[1, :, plain], row_in.at[1], inner, azi),
        halo(2, col_send.at[0], col_in.at[pl.ds(LANES - 8, 8)], rad, right),
        halo(3, col_send.at[1], col_in.at[pl.ds(0, 8)], rad, left),
        halo(4, row_send.at[0, :, corner], tile_in.at[0], outer, right),
        halo(5, row_send.at[0, :, corner], tile_in.at[1], outer, left),
        halo(6, row_send.at[1, :, corner], tile_in.at[2], inner, right),
        halo(7, row_send.at[1, :, corner], tile_in.at[3], inner, left),
    ]
    for one in halos:
        one.start()
    my_shift = shift[azi]
    col = iota((16, 256), 1)
    mode = 256 * (col % 16 // 2) + 128 * (col // 128) + 8 * iota((16, 256), 0) + col // 16 % 8
    phase = (2.0 * np.pi / NPHI) * ((mode * my_shift) & (NPHI - 1)).astype(F32)
    phase_cos, phase_sin = jnp.cos(phase), -jnp.sin(phase)
    for one in halos:
        one.wait_recv()

    sides = col_in[...].T
    lane_two = iota((2, LANES), 1)
    for m in range(MEMBERS):
        ext[m, pl.ds(0, SLAB), pl.ds(SEG, LANES)] = sides[SLAB * m : SLAB * (m + 1)]
    for m in range(MEMBERS):
        pair = pl.ds(2 * m, 2)
        for n, (at, edge_at, at_edge) in enumerate(
            ((EXT_R - 2, 0, rad == 0), (SLAB, SLAB - 1, rad == RAD - 1))
        ):
            edge = ext[m, pl.ds(edge_at, 1), :]
            far = jnp.where(lane_two < LANES // 2, tile_in[2 * n + 1, pair, :], tile_in[2 * n, pair, :])
            got = jnp.concatenate([row_in[n, pair, :], far], axis=1)
            ext[m, pl.ds(at, 2), :] = jnp.where(at_edge, jnp.broadcast_to(edge, (2, EXT_P)), got)

    coeffs = [wide(coef[n], EXT_P // LANES) for n in range(3)]
    for z in range(NZ):
        change, center = rates(lambda c, zz: ext[NZ * c + zz], z, EXT_R, coeffs)
        for c in range(3):
            sect[NZ * c + z] = center[c] + change[c]
    for m in range(MEMBERS):
        top = sect[m, pl.ds(0, 1), :]
        sect[m, pl.ds(EXT_R - 1, 1), :] = jnp.where(rad == 0, top, sect[m, pl.ds(EXT_R - 1, 1), :])
        low = sect[m, pl.ds(SLAB - 1, 1), :]
        sect[m, pl.ds(SLAB, 1), :] = jnp.where(rad == RAD - 1, low, sect[m, pl.ds(SLAB, 1), :])
    coeffs = [wide(coef[n, pl.ds(0, SLAB), :], EXT_P // LANES) for n in range(3)]
    weights = [weight[n] for n in range(4)]
    for z in range(NZ):
        change, center = rates(lambda c, zz: sect[NZ * c + zz], z, SLAB, coeffs)
        for c in range(3):
            m = NZ * c + z
            hydro = 0.5 * ext[m, pl.ds(0, SLAB), :] + 0.5 * (center[c] + change[c])
            ahead = pltpu.roll(hydro, EXT_P - 1, 1)
            behind = pltpu.roll(hydro, 1, 1)
            behind_two = pltpu.roll(hydro, 2, 1)
            for quad in range(QUADS):
                lanes = slice(LANES * quad, LANES * (quad + 1))
                moved = (
                    weights[0] * ahead[:, lanes] + weights[1] * hydro[:, lanes]
                    + weights[2] * behind[:, lanes] + weights[3] * behind_two[:, lanes]
                )
                for block in range(SLAB // 8):
                    move_out[pl.ds(8 * ROWS * block + MEMBERS * quad + m, 8, stride=ROWS), :] = moved[
                        8 * block : 8 * block + 8
                    ]
                if c == 0:
                    if z == 0:
                        total[:, lanes] = moved
                    else:
                        total[:, lanes] += moved
    for n in range(SLAB):
        for quad in range(QUADS):
            surf_out[n, quad, :] = total[n, LANES * quad : LANES * (quad + 1)]

    def to_azi(n, src, dst, step):
        return pltpu.make_async_remote_copy(
            src_ref=src, dst_ref=dst, send_sem=send_sem.at[n], recv_sem=recv_sem.at[n],
            device_id={"rad": rad, "azi": lax.rem(azi + step, AZI)}, device_id_type=MESH,
        )

    def to_rad(n, src, dst, step):
        return pltpu.make_async_remote_copy(
            src_ref=src, dst_ref=dst, send_sem=send_sem.at[n], recv_sem=recv_sem.at[n],
            device_id={"rad": lax.rem(rad + step, RAD), "azi": azi}, device_id_type=MESH,
        )

    def every(count, make):
        def one(step, carry):
            make(step).start()
            return carry

        lax.fori_loop(1, count, one, 0)

    def rows(index, size=ROWS):
        return pl.ds(pl.multiple_of(index * size, 8), size)

    def wait_all(n, ref, sem):
        pltpu.make_async_copy(ref, ref, sem.at[n]).wait()

    def target(step):
        return lax.rem(azi + step, AZI)

    def ring(step):
        return lax.rem(rad + step, RAD)

    every(AZI, lambda s: to_azi(0, surf_out.at[target(s)], surf_in.at[azi], s))
    surf_in[azi] = surf_out[azi]
    every(AZI, lambda s: to_azi(1, move_out.at[rows(target(s))], cycle_in.at[rows(azi)], s))
    cycle_in[rows(azi), :] = move_out[rows(azi), :]

    for load in loads[3:7]:
        load.wait()
    wait_all(0, surf_in.at[pl.ds(1, AZI - 1)], recv_sem)
    lines = surf_in[...].reshape(128, 128)
    halves = dot(t_first[...], lines)
    turn_cos, turn_sin = t_twiddle[:128], t_twiddle[128:]
    real, imag = halves[:128], halves[128:]
    joined = jnp.concatenate([real * turn_cos + imag * turn_sin, imag * turn_cos - real * turn_sin], axis=1)
    own = iota((128, 256), 0) % 8 == iota((128, 256), 1) // 16 % 8
    pick = (iota((16, 128), 1) // 8 == iota((16, 128), 0)).astype(F32)
    plain_modes = dot(pick, jnp.where(own, dot(joined, t_straight[...]), 0.0))
    turned_modes = dot(pick, jnp.where(own, dot(joined, t_turned[...]), 0.0))
    spectrum = (plain_modes * phase_cos + turned_modes * phase_sin).astype(jnp.bfloat16).astype(F32)
    for h in range(2):
        for q in range(16):
            spec_out[16 * h + q, 0, :] = spectrum[q, 128 * h : 128 * (h + 1)]
    every(AZI, lambda s: to_azi(2, spec_out.at[target(s)], spec_in.at[azi], s))
    spec_in[azi] = spec_out[azi]

    wait_all(1, cycle_in.at[pl.ds(0, ROWS * (AZI - 1))], recv_sem)
    cycle_in[pl.ds(ROWS * AZI, ROWS), :] = cycle_in[pl.ds(0, ROWS), :]
    turn_rows, turn_lanes = my_shift // LANES, my_shift % LANES
    lane = iota((ROWS, LANES), 1)

    def rotated(segment):
        start = lax.rem(QUADS * segment + LANES - 1 - turn_rows + LANES, LANES) * MEMBERS
        here = cycle_in[pl.ds(start + MEMBERS, ROWS), :]
        before = cycle_in[pl.ds(start, ROWS), :]
        return pltpu.roll(jnp.where(lane < LANES - turn_lanes, here, before), turn_lanes, 1)

    def rotate_and_send(step, carry):
        segment = target(step)
        cycle_out[rows(segment), :] = rotated(segment)
        to_azi(3, cycle_out.at[rows(segment)], move_in.at[rows(azi)], step).start()
        return carry

    lax.fori_loop(1, AZI, rotate_and_send, 0)
    move_in[rows(azi), :] = rotated(azi)

    wait_all(2, spec_in.at[pl.ds(1, AZI - 1)], recv_sem)
    modes_out[...] = spec_in[:, 0, :].astype(jnp.bfloat16)
    every(RAD, lambda s: to_rad(4, modes_out, modes_in.at[rad], s))
    modes_in[rad] = modes_out[...]
    wait_all(4, modes_in.at[pl.ds(1, RAD - 1)], recv_sem)
    columns = modes_in[...].reshape(NR, 128)
    loads[7].wait()
    out_lane = iota((NR, 128), 1)
    mine = out_lane % 16 // 2 == rad
    mode_potential = jnp.zeros((NR, 128), F32)
    for k in range(8):
        product = jnp.dot(kern[k], columns, preferred_element_type=F32)
        mode_potential = jnp.where(mine & (out_lane // 16 == k), product, mode_potential)
    pot_out[...] = mode_potential
    every(RAD, lambda s: to_rad(5, pot_out.at[rows(ring(s), SLAB)], pot_in.at[rad], s))
    pot_in[rad] = pot_out[rows(rad, SLAB), :]
    wait_all(5, pot_in.at[pl.ds(1, RAD - 1)], recv_sem)
    gathered = pot_in[0]
    for n in range(1, RAD):
        gathered = gathered + pot_in[n]
    for n in range(SLAB):
        back_out[n, 0, :] = gathered[n]
    every(AZI, lambda s: to_azi(6, back_out.at[target(s)], back_in.at[azi], s))
    back_in[azi] = back_out[azi]
    for load in loads[8:]:
        load.wait()
    wait_all(6, back_in.at[pl.ds(1, AZI - 1)], recv_sem)
    values = back_in[:, 0, :]
    values = jnp.concatenate([values[:16], values[16:]], axis=1)
    spread = (iota((128, 16), 0) // 8 == iota((128, 16), 1)).astype(F32)
    zero_mode = (iota((128, 256), 0) == 0) & (iota((128, 256), 1) < 2)
    values = jnp.where(own, dot(spread, values) * jnp.where(zero_mode, 1.0 / NPHI, 2.0 / NPHI), 0.0)
    pieces = dot(values, t_back[...])
    real, imag = pieces[:, :128], pieces[:, 128:]
    joined = jnp.concatenate([real * turn_cos - imag * turn_sin, real * turn_sin + imag * turn_cos], axis=0)
    potential[...] = dot(t_last[...], joined)

    wait_all(3, move_in.at[pl.ds(0, ROWS * (AZI - 1))], recv_sem)
    for c, out in enumerate((density_out, radial_out, azimuthal_out)):
        for z in range(NZ):
            for quad in range(QUADS):
                for block in range(SLAB // 8):
                    at = 8 * ROWS * block + MEMBERS * quad + NZ * c + z
                    out[z, pl.ds(8 * block, 8), pl.ds(LANES * quad, LANES)] = move_in[
                        pl.ds(at, 8, stride=ROWS), :
                    ]

    for one in halos:
        one.wait_send()
    wait_all(0, surf_in.at[pl.ds(1, AZI - 1)], send_sem)
    wait_all(1, cycle_in.at[pl.ds(0, ROWS * (AZI - 1))], send_sem)
    wait_all(2, spec_in.at[pl.ds(1, AZI - 1)], send_sem)
    wait_all(3, move_in.at[pl.ds(0, ROWS * (AZI - 1))], send_sem)
    wait_all(4, modes_in.at[pl.ds(1, RAD - 1)], send_sem)
    wait_all(5, pot_in.at[pl.ds(1, RAD - 1)], send_sem)
    wait_all(6, back_in.at[pl.ds(1, AZI - 1)], send_sem)


def step(density, radial_velocity, azimuthal_velocity, cycle_shift, remainder, kernel):
    whole = pl.BlockSpec(memory_space=pltpu.VMEM)
    away = pl.BlockSpec(memory_space=pl.ANY)
    scalars = pl.BlockSpec(memory_space=pltpu.SMEM)
    block = jax.ShapeDtypeStruct((NZ, SLAB, SEG), F32)
    moves = pltpu.VMEM((ROWS * AZI, LANES), F32)
    single = pltpu.VMEM((AZI, 1, LANES), F32)
    *moved, potential = pl.pallas_call(
        body,
        name="disc_step",
        out_shape=[block, block, block, jax.ShapeDtypeStruct((128, 128), F32)],
        in_specs=[away] * 3 + [scalars] * 2 + [away] * 7,
        out_specs=[whole] * 4,
        scratch_shapes=[
            pltpu.VMEM((MEMBERS, EXT_R, EXT_P), F32),
            pltpu.VMEM((MEMBERS, EXT_R, EXT_P), F32),
            pltpu.VMEM((3, EXT_R, LANES), F32),
            pltpu.VMEM((4, SLAB, LANES), F32),
            pltpu.VMEM((2, 2 * MEMBERS, EXT_P), F32),
            pltpu.VMEM((2, 2 * MEMBERS, SEG), F32),
            pltpu.VMEM((4, 2 * MEMBERS, LANES), F32),
            pltpu.VMEM((2, 8, MEMBERS * SLAB), F32),
            pltpu.VMEM((LANES, MEMBERS * SLAB), F32),
            moves,
            pltpu.VMEM((ROWS * (AZI + 1), LANES), F32),
            moves,
            moves,
            pltpu.VMEM((SLAB, SEG), F32),
            pltpu.VMEM((AZI, QUADS, LANES), F32),
            pltpu.VMEM((AZI, QUADS, LANES), F32),
            single,
            single,
            pltpu.VMEM((AZI, LANES), jnp.bfloat16),
            pltpu.VMEM((RAD, AZI, LANES), jnp.bfloat16),
            pltpu.VMEM((NR, LANES), F32),
            pltpu.VMEM((RAD, AZI, LANES), F32),
            single,
            single,
            pltpu.VMEM((8, NR, NR), jnp.bfloat16),
            pltpu.VMEM((256, 128), F32),
            pltpu.VMEM((128, 256), F32),
            pltpu.VMEM((256, 128), F32),
            pltpu.VMEM((256, 256), F32),
            pltpu.VMEM((256, 256), F32),
            pltpu.VMEM((256, 256), F32),
            pltpu.SemaphoreType.DMA((10,)),
            pltpu.SemaphoreType.DMA((8,)),
            pltpu.SemaphoreType.DMA((8,)),
            pltpu.SemaphoreType.DMA((7,)),
            pltpu.SemaphoreType.DMA((7,)),
        ],
        compiler_params=pltpu.CompilerParams(
            collective_id=0, has_side_effects=True, vmem_limit_bytes=40 * 1024 * 1024
        ),
    )(
        density, radial_velocity, azimuthal_velocity, cycle_shift, remainder, kernel,
        *[jnp.asarray(t) for t in tables()],
    )
    return *moved, potential.reshape(1, NPHI)


def solution(mesh):
    field = P(None, "rad", "azi")
    both = P(("rad", "azi"), None)
    return jax.shard_map(
        step,
        mesh=mesh,
        in_specs=(field, field, field, P("rad"), P("rad"), P(("rad", "azi"), None, None)),
        out_specs=(field, field, field, both),
        check_vma=False,
    )
```

profile of v0, /device:TPU:1, one launch (start us, length us, event | category | flops | bytes accessed | tf_op | source)
XLA Modules:
  0.0 74.7 jit_solution(18256247225538513918)
XLA Ops:
  0.6 0.0 copy-start
  0.6 1.2 %copy-done = bf16[8,256,256]{2,1,0:T(8,128)(2,1)S(1)} copy-done((bf16[8,256,256]{2,1,0:T(8,128)(2,1)S(1)}, bf16[8,256,256]{2,1,0:T(8,128)(2,1)}, u32[]{:S(2)}) %copy-start) | copy-done | bytes 1048600
  1.9 0.0 copy-start.1
  1.9 0.9 %copy-done.1 = f32[4,32,512]{2,1,0:T(8,128)S(1)} copy-done((f32[4,32,512]{2,1,0:T(8,128)S(1)}, f32[4,32,512]{2,1,0:T(8,128)}, u32[]{:S(2)}) %copy-start.1) | copy-done | bytes 262168
  2.8 0.0 copy-start.2
  2.8 0.9 %copy-done.2 = f32[4,32,512]{2,1,0:T(8,128)S(1)} copy-done((f32[4,32,512]{2,1,0:T(8,128)S(1)}, f32[4,32,512]{2,1,0:T(8,128)}, u32[]{:S(2)}) %copy-start.2) | copy-done | bytes 262168
  3.8 0.0 copy-start.3
  3.8 0.9 %copy-done.3 = f32[4,32,512]{2,1,0:T(8,128)S(1)} copy-done((f32[4,32,512]{2,1,0:T(8,128)S(1)}, f32[4,32,512]{2,1,0:T(8,128)}, u32[]{:S(2)}) %copy-start.3) | copy-done | bytes 262168
  4.7 0.0 copy-start.4
  4.7 0.9 %copy-done.4 = f32[256,256]{1,0:T(8,128)S(1)} copy-done((f32[256,256]{1,0:T(8,128)S(1)}, f32[256,256]{1,0:T(8,128)}, u32[]{:S(2)}) %copy-start.4) | copy-done | bytes 262168
  5.7 0.0 copy-start.5
  5.7 0.9 %copy-done.5 = f32[256,256]{1,0:T(8,128)S(1)} copy-done((f32[256,256]{1,0:T(8,128)S(1)}, f32[256,256]{1,0:T(8,128)}, u32[]{:S(2)}) %copy-start.5) | copy-done | bytes 262168
  6.6 0.0 copy-start.6
  6.6 0.9 %copy-done.6 = f32[256,256]{1,0:T(8,128)S(1)} copy-done((f32[256,256]{1,0:T(8,128)S(1)}, f32[256,256]{1,0:T(8,128)}, u32[]{:S(2)}) %copy-start.6) | copy-done | bytes 262168
  7.6 0.0 copy-start.7
  7.6 0.9 %copy-done.7 = f32[256,128]{1,0:T(8,128)S(1)} copy-done((f32[256,128]{1,0:T(8,128)S(1)}, f32[256,128]{1,0:T(8,128)}, u32[]{:S(2)}) %copy-start.7) | copy-done | bytes 131096
  8.5 0.0 copy-start.8
  8.5 0.9 %copy-done.8 = f32[128,256]{1,0:T(8,128)S(1)} copy-done((f32[128,256]{1,0:T(8,128)S(1)}, f32[128,256]{1,0:T(8,128)}, u32[]{:S(2)}) %copy-start.8) | copy-done | bytes 131096
  9.4 0.0 copy-start.9
  9.4 0.9 %copy-done.9 = f32[256,128]{1,0:T(8,128)S(1)} copy-done((f32[256,128]{1,0:T(8,128)S(1)}, f32[256,128]{1,0:T(8,128)}, u32[]{:S(2)}) %copy-start.9) | copy-done | bytes 131096
  10.3 0.0 copy-start.10
  10.3 0.7 copy-done.10
  10.9 0.0 copy-start.11
  10.9 0.7 copy-done.11
  11.6 60.4 %disc_step.1 = (f32[4,32,512]{2,1,0:T(8,128)S(1)}, f32[4,32,512]{2,1,0:T(8,128)S(1)}, f32[4,32,512]{2,1,0:T(8,128)S(1)}, f32[128,128]{1,0:T(8,128)S(1)}) custom-call(f32[4,32,512]{2,1,0:T(8,128)S(1)} %copy-done.1, f32[4,32,512]{2,1,0:T(8,128)S(1)} %copy-done.2, f32[4,32,512]{2,1,0:T(8,128)S(1)} %copy-done.3, s32[32]{0:T(128)S(1)} %copy-done.10, ...), custom_call_target="tpu_custom_call" | custom-call | tf_op jit(solution)/shard_map/disc_step/pallas_call | solution.py:399
  72.0 0.7 copy.20
  72.7 0.7 copy.21
  73.4 0.7 copy.22
  74.1 0.6 copy.23
Async XLA Ops:
  0.6 1.2 %copy-start = (bf16[8,256,256]{2,1,0:T(8,128)(2,1)S(1)}, bf16[8,256,256]{2,1,0:T(8,128)(2,1)}, u32[]{:S(2)}) copy-start(bf16[8,256,256]{2,1,0:T(8,128)(2,1)} %kernel.1) | copy-start | bytes 3145732
  1.9 0.9 %copy-start.1 = (f32[4,32,512]{2,1,0:T(8,128)S(1)}, f32[4,32,512]{2,1,0:T(8,128)}, u32[]{:S(2)}) copy-start(f32[4,32,512]{2,1,0:T(8,128)} %density.1) | copy-start | bytes 786436
  2.8 0.9 %copy-start.2 = (f32[4,32,512]{2,1,0:T(8,128)S(1)}, f32[4,32,512]{2,1,0:T(8,128)}, u32[]{:S(2)}) copy-start(f32[4,32,512]{2,1,0:T(8,128)} %radial_velocity.1) | copy-start | bytes 786436
  3.8 0.9 %copy-start.3 = (f32[4,32,512]{2,1,0:T(8,128)S(1)}, f32[4,32,512]{2,1,0:T(8,128)}, u32[]{:S(2)}) copy-start(f32[4,32,512]{2,1,0:T(8,128)} %azimuthal_velocity.1) | copy-start | bytes 786436
  4.7 0.9 %copy-start.4 = (f32[256,256]{1,0:T(8,128)S(1)}, f32[256,256]{1,0:T(8,128)}, u32[]{:S(2)}) copy-start(f32[256,256]{1,0:T(8,128)} %constant.17.clone.back) | copy-start | bytes 786436
  5.7 0.9 %copy-start.5 = (f32[256,256]{1,0:T(8,128)S(1)}, f32[256,256]{1,0:T(8,128)}, u32[]{:S(2)}) copy-start(f32[256,256]{1,0:T(8,128)} %constant.16.clone.turned) | copy-start | bytes 786436
  6.6 0.9 %copy-start.6 = (f32[256,256]{1,0:T(8,128)S(1)}, f32[256,256]{1,0:T(8,128)}, u32[]{:S(2)}) copy-start(f32[256,256]{1,0:T(8,128)} %constant.15.clone.straight) | copy-start | bytes 786436
  7.6 0.9 %copy-start.7 = (f32[256,128]{1,0:T(8,128)S(1)}, f32[256,128]{1,0:T(8,128)}, u32[]{:S(2)}) copy-start(f32[256,128]{1,0:T(8,128)} %constant.14.clone.twiddle) | copy-start | bytes 393220
  8.5 0.9 %copy-start.8 = (f32[128,256]{1,0:T(8,128)S(1)}, f32[128,256]{1,0:T(8,128)}, u32[]{:S(2)}) copy-start(f32[128,256]{1,0:T(8,128)} %constant.13.clone.last) | copy-start | bytes 393220
  9.4 0.9 %copy-start.9 = (f32[256,128]{1,0:T(8,128)S(1)}, f32[256,128]{1,0:T(8,128)}, u32[]{:S(2)}) copy-start(f32[256,128]{1,0:T(8,128)} %constant.12.clone.first) | copy-start | bytes 393220
  10.3 0.7 copy-start.10
  10.9 0.7 copy-start.11
where the time goes:
time: 75.1 us; the launch traced here: 74.7 us
  Pallas kernels  60.4 us (80%)
  local copies, waits for them, and re-layouts  13.7 us (18%)
    pallas_call x1, Pallas kernels, step(): pl.pallas_call(body, name='disc_step', out_shape=[block, block, block, ja...  60.4 us
    unnamed x28, local copies, waits for them, and re-layouts  13.7 us

commit v1 on v0

--- a/solution.py
+++ b/solution.py
@@ -36,17 +36,16 @@
     small = 2.0 * np.pi / NPHI * np.outer(n, n)
     twiddle = np.concatenate([np.cos(small), np.sin(small)], axis=0)
     col = np.arange(256)
-    half, ring, part = col // 128, col % 16 // 2, col % 2
+    half, ring, part = col // 128, col % 128 // 16, col % 2
     phi = 2.0 * np.pi / 128 * (np.outer(n, 2 * ring + half) % 128)
     cos, sin = np.cos(phi), np.sin(phi)
     real = part == 0
     straight = np.concatenate([np.where(real, cos, -sin), np.where(real, sin, cos)], axis=0)
-    turned = np.concatenate([np.where(real, sin, cos), np.where(real, -cos, sin)], axis=0)
     real = real[:, None]
     back = np.concatenate(
         [np.where(real, cos.T, -sin.T), np.where(real, sin.T, cos.T)], axis=1
     )
-    return [t.astype(np.float32) for t in (first, last, twiddle, straight, turned, back)]
+    return [t.astype(np.float32) for t in (first, last, twiddle, straight, back)]
 
 
 def dot(left, right):
@@ -96,12 +95,12 @@
 
 
 def body(
-    density, radial_velocity, azimuthal_velocity, shift, rest, kernel, first, last, twiddle, straight,
-    turned, back, density_out, radial_out, azimuthal_out, potential,
+    density, radial_velocity, azimuthal_velocity, shift_far, rest_far, kernel, first, last, twiddle, straight,
+    back, moved_out, potential,
     ext, sect, coef, weight, row_send, row_in, tile_in, col_send, col_in, move_out, cycle_in, cycle_out,
-    move_in, total, surf_out, surf_in, spec_out, spec_in, modes_out, modes_in, pot_out, pot_in, back_out,
-    back_in, kern, t_first, t_last, t_twiddle, t_straight, t_turned, t_back,
-    local_sem, halo_send, halo_recv, send_sem, recv_sem,
+    move_in, surf_out, surf_in, spec_out, spec_in, modes_out, modes_in, pot_out, pot_in, lines, back_out,
+    back_in, kern, t_first, t_last, t_twiddle, t_straight, t_back,
+    shift, rest, local_sem, halo_send, halo_recv, send_sem, recv_sem,
 ):
     rad, azi = lax.axis_index("rad"), lax.axis_index("azi")
     outer, inner = lax.rem(rad + 1, RAD), lax.rem(rad + RAD - 1, RAD)
@@ -113,8 +112,8 @@
     ]
     for n, (src, dst) in enumerate(
         (
-            (first, t_first), (twiddle, t_twiddle), (straight, t_straight), (turned, t_turned),
-            (kernel, kern), (back, t_back), (last, t_last),
+            (first, t_first), (twiddle, t_twiddle), (straight, t_straight),
+            (kernel, kern), (back, t_back), (last, t_last), (shift_far, shift), (rest_far, rest),
         )
     ):
         loads.append(pltpu.make_async_copy(src, dst, local_sem.at[3 + n]))
@@ -149,6 +148,8 @@
     coef[0] = 0.15 / radius
     coef[1] = 0.2 * steep
     coef[2] = 0.05 * steep
+    for load in loads[9:]:
+        load.wait()
     block_row = iota((8, LANES), 0)
     for block in range(SLAB // 8):
         fraction = jnp.zeros((8, LANES), F32)
@@ -174,6 +175,13 @@
     col_send[0] = columns[LANES - 8 :]
     col_send[1] = columns[:8]
 
+    for c in range(3):
+        heights = [ext[NZ * c + z, pl.ds(0, SLAB), pl.ds(0, SEG)] for z in range(NZ)]
+        total = (heights[0] + heights[1]) + (heights[2] + heights[3])
+        for n in range(SLAB):
+            for quad in range(QUADS):
+                surf_out[c, n, quad, :] = total[n, LANES * quad : LANES * (quad + 1)]
+
     pl.semaphore_wait(barrier, AZI - 1 + RAD - 1 + 4)
 
     def halo(n, src, dst, r_to, a_to):
@@ -195,11 +203,72 @@
     ]
     for one in halos:
         one.start()
-    my_shift = shift[azi]
-    col = iota((16, 256), 1)
-    mode = 256 * (col % 16 // 2) + 128 * (col // 128) + 8 * iota((16, 256), 0) + col // 16 % 8
-    phase = (2.0 * np.pi / NPHI) * ((mode * my_shift) & (NPHI - 1)).astype(F32)
-    phase_cos, phase_sin = jnp.cos(phase), -jnp.sin(phase)
+    finish = [one.wait_send for one in halos]
+    def to_azi(n, src, dst, step):
+        return pltpu.make_async_remote_copy(
+            src_ref=src, dst_ref=dst, send_sem=send_sem.at[n], recv_sem=recv_sem.at[n],
+            device_id={"rad": rad, "azi": lax.rem(azi + step, AZI)}, device_id_type=MESH,
+        )
+
+    def to_rad(n, src, dst, step):
+        return pltpu.make_async_remote_copy(
+            src_ref=src, dst_ref=dst, send_sem=send_sem.at[n], recv_sem=recv_sem.at[n],
+            device_id={"rad": lax.rem(rad + step, RAD), "azi": azi}, device_id_type=MESH,
+        )
+
+    def every(count, make):
+        def one(step, carry):
+            make(step).start()
+            return carry
+
+        lax.fori_loop(1, count, one, 0)
+
+    def rows(index, size=ROWS):
+        return pl.ds(pl.multiple_of(index * size, 8), size)
+
+    def wait_all(n, ref, sem):
+        pltpu.make_async_copy(ref, ref, sem.at[n]).wait()
+
+    def later(n, ref):
+        finish.append(lambda: wait_all(n, ref, send_sem))
+
+    def target(step):
+        return lax.rem(azi + step, AZI)
+
+    def ring(step):
+        return lax.rem(rad + step, RAD)
+
+    every(AZI, lambda s: to_azi(0, surf_out.at[:, target(s)], surf_in.at[:, azi], s))
+    later(0, surf_in.at[:, pl.ds(1, AZI - 1)])
+    for c in range(3):
+        surf_in[c, azi] = surf_out[c, azi]
+
+    for load in loads[3:6]:
+        load.wait()
+    wait_all(0, surf_in.at[:, pl.ds(1, AZI - 1)], recv_sem)
+    sums = jnp.concatenate([surf_in[c].reshape(128, 128) for c in range(3)], axis=1)
+    halves = dot(t_first[...], sums)
+    joined = []
+    for c in range(3):
+        turn_cos, turn_sin = t_twiddle[:128], t_twiddle[128:]
+        real, imag = halves[:128, 128 * c : 128 * (c + 1)], halves[128:, 128 * c : 128 * (c + 1)]
+        joined.append(
+            jnp.concatenate([real * turn_cos + imag * turn_sin, imag * turn_cos - real * turn_sin], axis=1)
+        )
+    modes = dot(jnp.concatenate(joined, axis=0), t_straight[...])
+    own = iota((384, 256), 0) % 8 == iota((384, 256), 1) // 2 % 8
+    pick = (iota((48, 384), 1) // 8 == iota((48, 384), 0)).astype(F32)
+    modes = dot(pick, jnp.where(own, modes, 0.0))
+    note = jnp.where(iota((1, LANES), 1) % 2 == 0, shift[azi].astype(F32), rest[azi])
+    for h in range(2):
+        for q in range(16):
+            for c in range(3):
+                spec_out[16 * h + q, c, :] = modes[16 * c + q, 128 * h : 128 * (h + 1)]
+            spec_out[16 * h + q, 3, :] = note[0]
+    every(AZI, lambda s: to_azi(2, spec_out.at[target(s)], spec_in.at[azi], s))
+    later(2, spec_in.at[pl.ds(1, AZI - 1)])
+    spec_in[azi] = spec_out[azi]
+
     for one in halos:
         one.wait_recv()
 
@@ -247,72 +316,27 @@
                     move_out[pl.ds(8 * ROWS * block + MEMBERS * quad + m, 8, stride=ROWS), :] = moved[
                         8 * block : 8 * block + 8
                     ]
-                if c == 0:
-                    if z == 0:
-                        total[:, lanes] = moved
-                    else:
-                        total[:, lanes] += moved
-    for n in range(SLAB):
-        for quad in range(QUADS):
-            surf_out[n, quad, :] = total[n, LANES * quad : LANES * (quad + 1)]
-
-    def to_azi(n, src, dst, step):
-        return pltpu.make_async_remote_copy(
-            src_ref=src, dst_ref=dst, send_sem=send_sem.at[n], recv_sem=recv_sem.at[n],
-            device_id={"rad": rad, "azi": lax.rem(azi + step, AZI)}, device_id_type=MESH,
-        )
-
-    def to_rad(n, src, dst, step):
-        return pltpu.make_async_remote_copy(
-            src_ref=src, dst_ref=dst, send_sem=send_sem.at[n], recv_sem=recv_sem.at[n],
-            device_id={"rad": lax.rem(rad + step, RAD), "azi": azi}, device_id_type=MESH,
-        )
-
-    def every(count, make):
-        def one(step, carry):
-            make(step).start()
-            return carry
-
-        lax.fori_loop(1, count, one, 0)
-
-    def rows(index, size=ROWS):
-        return pl.ds(pl.multiple_of(index * size, 8), size)
-
-    def wait_all(n, ref, sem):
-        pltpu.make_async_copy(ref, ref, sem.at[n]).wait()
-
-    def target(step):
-        return lax.rem(azi + step, AZI)
-
-    def ring(step):
-        return lax.rem(rad + step, RAD)
-
-    every(AZI, lambda s: to_azi(0, surf_out.at[target(s)], surf_in.at[azi], s))
-    surf_in[azi] = surf_out[azi]
+
     every(AZI, lambda s: to_azi(1, move_out.at[rows(target(s))], cycle_in.at[rows(azi)], s))
+    later(1, cycle_in.at[pl.ds(0, ROWS * (AZI - 1))])
     cycle_in[rows(azi), :] = move_out[rows(azi), :]
 
-    for load in loads[3:7]:
-        load.wait()
-    wait_all(0, surf_in.at[pl.ds(1, AZI - 1)], recv_sem)
-    lines = surf_in[...].reshape(128, 128)
-    halves = dot(t_first[...], lines)
-    turn_cos, turn_sin = t_twiddle[:128], t_twiddle[128:]
-    real, imag = halves[:128], halves[128:]
-    joined = jnp.concatenate([real * turn_cos + imag * turn_sin, imag * turn_cos - real * turn_sin], axis=1)
-    own = iota((128, 256), 0) % 8 == iota((128, 256), 1) // 16 % 8
-    pick = (iota((16, 128), 1) // 8 == iota((16, 128), 0)).astype(F32)
-    plain_modes = dot(pick, jnp.where(own, dot(joined, t_straight[...]), 0.0))
-    turned_modes = dot(pick, jnp.where(own, dot(joined, t_turned[...]), 0.0))
-    spectrum = (plain_modes * phase_cos + turned_modes * phase_sin).astype(jnp.bfloat16).astype(F32)
-    for h in range(2):
-        for q in range(16):
-            spec_out[16 * h + q, 0, :] = spectrum[q, 128 * h : 128 * (h + 1)]
-    every(AZI, lambda s: to_azi(2, spec_out.at[target(s)], spec_in.at[azi], s))
-    spec_in[azi] = spec_out[azi]
+    wait_all(2, spec_in.at[pl.ds(1, AZI - 1)], recv_sem)
+    tile_lane = iota((AZI // 2, LANES), 1) // 16
+    parts = [spec_in[pl.ds(16 * h, 16), c, :] for h in range(2) for c in range(4)]
+    for n in range(RAD):
+        packed = parts[0] if n == 0 else pltpu.roll(parts[0], LANES - 16 * n, 1)
+        for at in range(1, 8):
+            turn = 16 * (at - n) % LANES
+            packed = jnp.where(tile_lane == at, pltpu.roll(parts[at], turn, 1) if turn else parts[at], packed)
+        modes_out[n] = packed
+    every(RAD, lambda s: to_rad(4, modes_out.at[ring(s)], modes_in.at[rad], s))
+    later(4, modes_in.at[pl.ds(1, RAD - 1)])
+    modes_in[rad] = modes_out[rad]
 
     wait_all(1, cycle_in.at[pl.ds(0, ROWS * (AZI - 1))], recv_sem)
     cycle_in[pl.ds(ROWS * AZI, ROWS), :] = cycle_in[pl.ds(0, ROWS), :]
+    my_shift = shift[azi]
     turn_rows, turn_lanes = my_shift // LANES, my_shift % LANES
     lane = iota((ROWS, LANES), 1)
 
@@ -329,46 +353,99 @@
         return carry
 
     lax.fori_loop(1, AZI, rotate_and_send, 0)
+    later(3, move_in.at[pl.ds(0, ROWS * (AZI - 1))])
     move_in[rows(azi), :] = rotated(azi)
 
-    wait_all(2, spec_in.at[pl.ds(1, AZI - 1)], recv_sem)
-    modes_out[...] = spec_in[:, 0, :].astype(jnp.bfloat16)
-    every(RAD, lambda s: to_rad(4, modes_out, modes_in.at[rad], s))
-    modes_in[rad] = modes_out[...]
+    shape = (16, NR)
+    mode = 256 * rad + 8 * azi + iota(shape, 0) // 2
+    part = iota(shape, 0) % 2
+    at_cycle = iota(shape, 1)
+    theta = (2.0 * np.pi / NPHI) * mode.astype(F32)
+    wave_cos, wave_sin = jnp.cos(theta), jnp.sin(theta)
+    double_cos, double_sin = jnp.cos(2.0 * theta), jnp.sin(2.0 * theta)
+    cycle_radius = 1.0 + 4.0 * (at_cycle.astype(F32) + 0.5) / NR
+    cycle_steep = 1.0 / (cycle_radius * jnp.sqrt(cycle_radius))
+    courant, coriolis, epicycle = 0.3 / cycle_radius, 0.2 * cycle_steep, 0.05 * cycle_steep
+    drift = courant * wave_sin
+    bend = 2.0 * wave_cos - 2.0
+
+    def times_i(value):
+        return jnp.where(part == 0, -pltpu.roll(value, 15, 0), pltpu.roll(value, 1, 0))
+
+    def neighbours(value):
+        behind = jnp.where(at_cycle == 0, value, pltpu.roll(value, 1, 1))
+        ahead = jnp.where(at_cycle == NR - 1, value, pltpu.roll(value, NR - 1, 1))
+        return 0.5 * (ahead - behind), (ahead + behind - 2.0 * value) + bend * value
+
+    loads[6].wait()
     wait_all(4, modes_in.at[pl.ds(1, RAD - 1)], recv_sem)
-    columns = modes_in[...].reshape(NR, 128)
-    loads[7].wait()
-    out_lane = iota((NR, 128), 1)
-    mine = out_lane % 16 // 2 == rad
-    mode_potential = jnp.zeros((NR, 128), F32)
+    arrived = []
+    for n in range(RAD):
+        arrived += [modes_in[n], pltpu.roll(modes_in[n], LANES // 2, 1)]
+    arrived = jnp.concatenate(arrived, axis=0).T
+    rho, ur, up, extra = [arrived[16 * c : 16 * (c + 1)] for c in range(4)]
+    cycle_turn = jnp.where(part == 0, extra, pltpu.roll(extra, 1, 0)).astype(jnp.int32)
+    fraction = jnp.where(part == 0, pltpu.roll(extra, 15, 0), extra)
+    phase = (2.0 * np.pi / NPHI) * ((mode * cycle_turn) & (NPHI - 1)).astype(F32)
+    phase_cos, phase_sin = jnp.cos(phase), jnp.sin(phase)
+    w_next, w_here, w_prev, w_prev_two = cubic_weights(fraction)
+    mix_real = (w_next + w_prev) * wave_cos + w_here + w_prev_two * double_cos
+    mix_imag = (w_next - w_prev) * wave_sin - w_prev_two * double_sin
+    turn_real = mix_real * phase_cos + mix_imag * phase_sin
+    turn_imag = mix_imag * phase_cos - mix_real * phase_sin
+    rho_diff, rho_spread = neighbours(rho)
+    ur_diff, ur_spread = neighbours(ur)
+    rho_one = rho - (RADIAL_COURANT * ur_diff + drift * times_i(up)) + VISCOSITY * rho_spread
+    ur_one = ur + coriolis * up - RADIAL_COURANT * rho_diff + VISCOSITY * ur_spread
+    up_one = up - epicycle * ur - drift * times_i(rho) + VISCOSITY * neighbours(up)[1]
+    change = VISCOSITY * neighbours(rho_one)[1] - (
+        RADIAL_COURANT * neighbours(ur_one)[0] + drift * times_i(up_one)
+    )
+    surface = 0.5 * rho + 0.5 * (rho_one + change)
+    spectrum = (turn_real * surface + turn_imag * times_i(surface)).astype(jnp.bfloat16)
+
+    mode_potential = jnp.zeros(shape, F32)
     for k in range(8):
-        product = jnp.dot(kern[k], columns, preferred_element_type=F32)
-        mode_potential = jnp.where(mine & (out_lane // 16 == k), product, mode_potential)
-    pot_out[...] = mode_potential
-    every(RAD, lambda s: to_rad(5, pot_out.at[rows(ring(s), SLAB)], pot_in.at[rad], s))
-    pot_in[rad] = pot_out[rows(rad, SLAB), :]
+        product = lax.dot_general(
+            spectrum, kern[k], (((1,), (1,)), ((), ())), preferred_element_type=F32
+        )
+        mode_potential = jnp.where(iota(shape, 0) // 2 == k, product, mode_potential)
+    for h in range(2):
+        pot_out[h] = mode_potential[:, LANES * h : LANES * (h + 1)]
+    every(RAD, lambda s: to_rad(5, pot_out.at[ring(s) // 4], pot_in.at[rad], s))
+    later(5, pot_in.at[pl.ds(1, RAD - 1)])
+    pot_in[rad] = pot_out[rad // 4]
     wait_all(5, pot_in.at[pl.ds(1, RAD - 1)], recv_sem)
-    gathered = pot_in[0]
-    for n in range(1, RAD):
-        gathered = gathered + pot_in[n]
+    lines[...] = pot_in[...].reshape(LANES, LANES).T
+    gathered = lines[rows(lax.rem(rad, 4), SLAB), :]
     for n in range(SLAB):
         back_out[n, 0, :] = gathered[n]
     every(AZI, lambda s: to_azi(6, back_out.at[target(s)], back_in.at[azi], s))
+    later(6, back_in.at[pl.ds(1, AZI - 1)])
     back_in[azi] = back_out[azi]
-    for load in loads[8:]:
+    for load in loads[7:9]:
         load.wait()
     wait_all(6, back_in.at[pl.ds(1, AZI - 1)], recv_sem)
     values = back_in[:, 0, :]
     values = jnp.concatenate([values[:16], values[16:]], axis=1)
     spread = (iota((128, 16), 0) // 8 == iota((128, 16), 1)).astype(F32)
     zero_mode = (iota((128, 256), 0) == 0) & (iota((128, 256), 1) < 2)
+    own = iota((128, 256), 0) % 8 == iota((128, 256), 1) // 2 % 8
     values = jnp.where(own, dot(spread, values) * jnp.where(zero_mode, 1.0 / NPHI, 2.0 / NPHI), 0.0)
     pieces = dot(values, t_back[...])
     real, imag = pieces[:, :128], pieces[:, 128:]
+    turn_cos, turn_sin = t_twiddle[:128], t_twiddle[128:]
     joined = jnp.concatenate([real * turn_cos - imag * turn_sin, real * turn_sin + imag * turn_cos], axis=0)
     potential[...] = dot(t_last[...], joined)
 
     wait_all(3, move_in.at[pl.ds(0, ROWS * (AZI - 1))], recv_sem)
+    moved_out[...] = move_in[...]
+
+    for wait in finish:
+        wait()
+
+
+def unpack(move_in, lines, density_out, radial_out, azimuthal_out, potential):
     for c, out in enumerate((density_out, radial_out, azimuthal_out)):
         for z in range(NZ):
             for quad in range(QUADS):
@@ -377,31 +454,21 @@
                     out[z, pl.ds(8 * block, 8), pl.ds(LANES * quad, LANES)] = move_in[
                         pl.ds(at, 8, stride=ROWS), :
                     ]
-
-    for one in halos:
-        one.wait_send()
-    wait_all(0, surf_in.at[pl.ds(1, AZI - 1)], send_sem)
-    wait_all(1, cycle_in.at[pl.ds(0, ROWS * (AZI - 1))], send_sem)
-    wait_all(2, spec_in.at[pl.ds(1, AZI - 1)], send_sem)
-    wait_all(3, move_in.at[pl.ds(0, ROWS * (AZI - 1))], send_sem)
-    wait_all(4, modes_in.at[pl.ds(1, RAD - 1)], send_sem)
-    wait_all(5, pot_in.at[pl.ds(1, RAD - 1)], send_sem)
-    wait_all(6, back_in.at[pl.ds(1, AZI - 1)], send_sem)
+    potential[...] = lines[...]
 
 
 def step(density, radial_velocity, azimuthal_velocity, cycle_shift, remainder, kernel):
     whole = pl.BlockSpec(memory_space=pltpu.VMEM)
-    away = pl.BlockSpec(memory_space=pl.ANY)
-    scalars = pl.BlockSpec(memory_space=pltpu.SMEM)
+    away = pl.BlockSpec(memory_space=pltpu.HBM)
     block = jax.ShapeDtypeStruct((NZ, SLAB, SEG), F32)
     moves = pltpu.VMEM((ROWS * AZI, LANES), F32)
     single = pltpu.VMEM((AZI, 1, LANES), F32)
-    *moved, potential = pl.pallas_call(
+    moved, lines = pl.pallas_call(
         body,
         name="disc_step",
-        out_shape=[block, block, block, jax.ShapeDtypeStruct((128, 128), F32)],
-        in_specs=[away] * 3 + [scalars] * 2 + [away] * 7,
-        out_specs=[whole] * 4,
+        out_shape=[jax.ShapeDtypeStruct((ROWS * AZI, LANES), F32), jax.ShapeDtypeStruct((128, 128), F32)],
+        in_specs=[away] * 11,
+        out_specs=[whole] * 2,
         scratch_shapes=[
             pltpu.VMEM((MEMBERS, EXT_R, EXT_P), F32),
             pltpu.VMEM((MEMBERS, EXT_R, EXT_P), F32),
@@ -416,15 +483,15 @@
             pltpu.VMEM((ROWS * (AZI + 1), LANES), F32),
             moves,
             moves,
-            pltpu.VMEM((SLAB, SEG), F32),
-            pltpu.VMEM((AZI, QUADS, LANES), F32),
-            pltpu.VMEM((AZI, QUADS, LANES), F32),
-            single,
-            single,
-            pltpu.VMEM((AZI, LANES), jnp.bfloat16),
-            pltpu.VMEM((RAD, AZI, LANES), jnp.bfloat16),
-            pltpu.VMEM((NR, LANES), F32),
-            pltpu.VMEM((RAD, AZI, LANES), F32),
+            pltpu.VMEM((3, AZI, QUADS, LANES), F32),
+            pltpu.VMEM((3, AZI, QUADS, LANES), F32),
+            pltpu.VMEM((AZI, 4, LANES), F32),
+            pltpu.VMEM((AZI, 4, LANES), F32),
+            pltpu.VMEM((RAD, AZI // 2, LANES), F32),
+            pltpu.VMEM((RAD, AZI // 2, LANES), F32),
+            pltpu.VMEM((2, 16, LANES), F32),
+            pltpu.VMEM((RAD, 16, LANES), F32),
+            pltpu.VMEM((LANES, LANES), F32),
             single,
             single,
             pltpu.VMEM((8, NR, NR), jnp.bfloat16),
@@ -433,8 +500,9 @@
             pltpu.VMEM((256, 128), F32),
             pltpu.VMEM((256, 256), F32),
             pltpu.VMEM((256, 256), F32),
-            pltpu.VMEM((256, 256), F32),
-            pltpu.SemaphoreType.DMA((10,)),
+            pltpu.SMEM((SLAB,), jnp.int32),
+            pltpu.SMEM((SLAB,), F32),
+            pltpu.SemaphoreType.DMA((11,)),
             pltpu.SemaphoreType.DMA((8,)),
             pltpu.SemaphoreType.DMA((8,)),
             pltpu.SemaphoreType.DMA((7,)),
@@ -444,10 +512,23 @@
             collective_id=0, has_side_effects=True, vmem_limit_bytes=40 * 1024 * 1024
         ),
     )(
-        density, radial_velocity, azimuthal_velocity, cycle_shift, remainder, kernel,
-        *[jnp.asarray(t) for t in tables()],
+        *[
+            pltpu.with_memory_space_constraint(value, pltpu.HBM)
+            for value in (
+                density, radial_velocity, azimuthal_velocity, cycle_shift, remainder, kernel,
+                *[jnp.asarray(table) for table in tables()],
+            )
+        ]
     )
-    return *moved, potential.reshape(1, NPHI)
+    *fields, potential = pl.pallas_call(
+        unpack,
+        name="unpack",
+        out_shape=[block, block, block, jax.ShapeDtypeStruct((128, 128), F32)],
+        in_specs=[whole] * 2,
+        out_specs=[whole] * 4,
+        compiler_params=pltpu.CompilerParams(vmem_limit_bytes=8 * 1024 * 1024),
+    )(moved, lines)
+    return *fields, potential.reshape(1, NPHI)
 
 
 def solution(mesh):

time: 75.1 us -> 56.4 us (0.75)
  local copies, waits for them, and re-layouts: 13.7 us -> 0 us
  Pallas kernels: 60.4 us -> 55.7 us
    unnamed x28 -> x0, local copies, waits for them, and re-layouts: 13.7 us -> none
    pallas_call x1 -> x2, Pallas kernels: 60.4 us -> 55.7 us  [the longest x1 54.6 us: step(): pl.pallas_call(body, name='disc_step', out_shape=[jax.ShapeDtypeStruct((R...]
where the time goes in v1:
time: 56.4 us; the launch traced here: 56.3 us
  Pallas kernels  55.7 us (99%)
  between operations  0.64 us (1%)
    pallas_call x1, Pallas kernels, step(): pl.pallas_call(body, name='disc_step', out_shape=[jax.ShapeDtypeStruct((R...  54.6 us
    pallas_call x1, Pallas kernels, step(): pl.pallas_call(unpack, name='unpack', out_shape=[block, block, block, jax...  1.13 us

profile of v1, /device:TPU:1, one launch (start us, length us, event | category | flops | bytes accessed | tf_op | source)
XLA Modules:
  0.0 56.3 jit_solution(5529753501758136987)
XLA Ops:
  0.6 54.6 %disc_step.1 = (f32[1536,128]{1,0:T(8,128)S(1)}, f32[128,128]{1,0:T(8,128)S(1)}) custom-call(f32[4,32,512]{2,1,0:T(8,128)} %density.1, f32[4,32,512]{2,1,0:T(8,128)} %radial_velocity.1, f32[4,32,512]{2,1,0:T(8,128)} %azimuthal_velocity.1, s32[32]{0:T(128)} %shift_far.1, f32[32]{0:T(128)} %rest_far.1, bf16[8,256,256]{2,1,0:T(8,128)(2,1)} %kernel.1, ...), custom_call_target="tpu_custom_call" | custom-call | tf_op jit(solution)/shard_map/disc_step/pallas_call | solution.py:466
  55.2 1.1 %unpack.1 = (f32[4,32,512]{2,1,0:T(8,128)}, f32[4,32,512]{2,1,0:T(8,128)}, f32[4,32,512]{2,1,0:T(8,128)}, f32[128,128]{1,0:T(8,128)}) custom-call(f32[1536,128]{1,0:T(8,128)S(1)} %get-tuple-element.10.move_in, f32[128,128]{1,0:T(8,128)S(1)} %get-tuple-element.11.lines), custom_call_target="tpu_custom_call" | custom-call | tf_op jit(solution)/shard_map/unpack/pallas_call | solution.py:523

commit v2 on v1

--- a/solution.py
+++ b/solution.py
@@ -18,7 +18,11 @@
 LANES = 128
 QUADS = SEG // LANES
 MEMBERS = 3 * NZ
-ROWS = MEMBERS * QUADS
+WORDS = MEMBERS // 2
+ROWS = WORDS * QUADS
+CODES = 32767
+OCTAVES = 28.0
+TOP = 4.0
 EXT_R = SLAB + 8
 EXT_P = SEG + LANES
 RADIAL_COURANT = 0.3
@@ -67,6 +71,18 @@
     w_prev = (moved - 1.0) * moved * (moved + 2.0) / 2.0
     w_prev_two = -(moved - 1.0) * moved * (moved + 1.0) / 6.0
     return w_next, w_here, w_prev, w_prev_two
+
+
+def encode(value):
+    level = (jnp.log(jnp.abs(value)) * (1.0 / np.log(2.0)) - TOP) * (CODES / OCTAVES) + (CODES + 0.5)
+    code = jnp.clip(level, 0.0, CODES + 0.5).astype(jnp.int32)
+    return jnp.where(value < 0, -code, code)
+
+
+def decode(code):
+    level = (jnp.abs(code) - CODES).astype(F32) * (OCTAVES / CODES) + TOP
+    size = jnp.where(code == 0, 0.0, jnp.exp(level * np.log(2.0)))
+    return jnp.where(code < 0, -size, size)
 
 
 def rates(get, z, rows, coeffs):
@@ -298,6 +314,7 @@
         sect[m, pl.ds(SLAB, 1), :] = jnp.where(rad == RAD - 1, low, sect[m, pl.ds(SLAB, 1), :])
     coeffs = [wide(coef[n, pl.ds(0, SLAB), :], EXT_P // LANES) for n in range(3)]
     weights = [weight[n] for n in range(4)]
+    lower = {}
     for z in range(NZ):
         change, center = rates(lambda c, zz: sect[NZ * c + zz], z, SLAB, coeffs)
         for c in range(3):
@@ -312,10 +329,14 @@
                     weights[0] * ahead[:, lanes] + weights[1] * hydro[:, lanes]
                     + weights[2] * behind[:, lanes] + weights[3] * behind_two[:, lanes]
                 )
+                code = encode(moved)
+                if z % 2 == 0:
+                    lower[c, quad] = code & 0xFFFF
+                    continue
+                words = (code << 16) | lower[c, quad]
                 for block in range(SLAB // 8):
-                    move_out[pl.ds(8 * ROWS * block + MEMBERS * quad + m, 8, stride=ROWS), :] = moved[
-                        8 * block : 8 * block + 8
-                    ]
+                    at = 8 * ROWS * block + WORDS * quad + 2 * c + z // 2
+                    move_out[pl.ds(at, 8, stride=ROWS), :] = words[8 * block : 8 * block + 8]
 
     every(AZI, lambda s: to_azi(1, move_out.at[rows(target(s))], cycle_in.at[rows(azi)], s))
     later(1, cycle_in.at[pl.ds(0, ROWS * (AZI - 1))])
@@ -341,8 +362,8 @@
     lane = iota((ROWS, LANES), 1)
 
     def rotated(segment):
-        start = lax.rem(QUADS * segment + LANES - 1 - turn_rows + LANES, LANES) * MEMBERS
-        here = cycle_in[pl.ds(start + MEMBERS, ROWS), :]
+        start = lax.rem(QUADS * segment + LANES - 1 - turn_rows + LANES, LANES) * WORDS
+        here = cycle_in[pl.ds(start + WORDS, ROWS), :]
         before = cycle_in[pl.ds(start, ROWS), :]
         return pltpu.roll(jnp.where(lane < LANES - turn_lanes, here, before), turn_lanes, 1)
 
@@ -447,13 +468,14 @@
 
 def unpack(move_in, lines, density_out, radial_out, azimuthal_out, potential):
     for c, out in enumerate((density_out, radial_out, azimuthal_out)):
-        for z in range(NZ):
+        for pair in range(NZ // 2):
             for quad in range(QUADS):
                 for block in range(SLAB // 8):
-                    at = 8 * ROWS * block + MEMBERS * quad + NZ * c + z
-                    out[z, pl.ds(8 * block, 8), pl.ds(LANES * quad, LANES)] = move_in[
-                        pl.ds(at, 8, stride=ROWS), :
-                    ]
+                    at = 8 * ROWS * block + WORDS * quad + 2 * c + pair
+                    words = move_in[pl.ds(at, 8, stride=ROWS), :]
+                    place = pl.ds(8 * block, 8), pl.ds(LANES * quad, LANES)
+                    out[2 * pair, *place] = decode((words << 16) >> 16)
+                    out[2 * pair + 1, *place] = decode(words >> 16)
     potential[...] = lines[...]
 
 
@@ -461,12 +483,12 @@
     whole = pl.BlockSpec(memory_space=pltpu.VMEM)
     away = pl.BlockSpec(memory_space=pltpu.HBM)
     block = jax.ShapeDtypeStruct((NZ, SLAB, SEG), F32)
-    moves = pltpu.VMEM((ROWS * AZI, LANES), F32)
+    moves = pltpu.VMEM((ROWS * AZI, LANES), jnp.int32)
     single = pltpu.VMEM((AZI, 1, LANES), F32)
     moved, lines = pl.pallas_call(
         body,
         name="disc_step",
-        out_shape=[jax.ShapeDtypeStruct((ROWS * AZI, LANES), F32), jax.ShapeDtypeStruct((128, 128), F32)],
+        out_shape=[jax.ShapeDtypeStruct((ROWS * AZI, LANES), jnp.int32), jax.ShapeDtypeStruct((128, 128), F32)],
         in_specs=[away] * 11,
         out_specs=[whole] * 2,
         scratch_shapes=[
@@ -480,7 +502,7 @@
             pltpu.VMEM((2, 8, MEMBERS * SLAB), F32),
             pltpu.VMEM((LANES, MEMBERS * SLAB), F32),
             moves,
-            pltpu.VMEM((ROWS * (AZI + 1), LANES), F32),
+            pltpu.VMEM((ROWS * (AZI + 1), LANES), jnp.int32),
             moves,
             moves,
             pltpu.VMEM((3, AZI, QUADS, LANES), F32),

time: 56.4 us -> 47.6 us (0.84)
  Pallas kernels: 55.7 us -> 46.9 us
    pallas_call x1, Pallas kernels: 54.6 us -> 45.7 us  [step(): pl.pallas_call(body, name='disc_step', out_shape=[jax.ShapeDtypeStruct((R...]
where the time goes in v2:
time: 47.6 us; the launch traced here: 47.5 us
  Pallas kernels  46.9 us (99%)
  between operations  0.64 us (1%)
    pallas_call x1, Pallas kernels, step(): pl.pallas_call(body, name='disc_step', out_shape=[jax.ShapeDtypeStruct((R...  45.7 us
    pallas_call x1, Pallas kernels, step(): pl.pallas_call(unpack, name='unpack', out_shape=[block, block, block, jax...  1.12 us

profile of v2, /device:TPU:1, one launch (start us, length us, event | category | flops | bytes accessed | tf_op | source)
XLA Modules:
  0.0 47.5 jit_solution(6616417348950298734)
XLA Ops:
  0.6 45.7 %disc_step.1 = (s32[768,128]{1,0:T(8,128)S(1)}, f32[128,128]{1,0:T(8,128)S(1)}) custom-call(f32[4,32,512]{2,1,0:T(8,128)} %density.1, f32[4,32,512]{2,1,0:T(8,128)} %radial_velocity.1, f32[4,32,512]{2,1,0:T(8,128)} %azimuthal_velocity.1, s32[32]{0:T(128)} %shift_far.1, f32[32]{0:T(128)} %rest_far.1, bf16[8,256,256]{2,1,0:T(8,128)(2,1)} %kernel.1, ...), custom_call_target="tpu_custom_call" | custom-call | tf_op jit(solution)/shard_map/disc_step/pallas_call | solution.py:488
  46.4 1.1 %unpack.1 = (f32[4,32,512]{2,1,0:T(8,128)}, f32[4,32,512]{2,1,0:T(8,128)}, f32[4,32,512]{2,1,0:T(8,128)}, f32[128,128]{1,0:T(8,128)}) custom-call(s32[768,128]{1,0:T(8,128)S(1)} %get-tuple-element.10.move_in, f32[128,128]{1,0:T(8,128)S(1)} %get-tuple-element.11.lines), custom_call_target="tpu_custom_call" | custom-call | tf_op jit(solution)/shard_map/unpack/pallas_call | solution.py:545

commit v3 on v2

--- a/solution.py
+++ b/solution.py
@@ -20,6 +20,7 @@
 MEMBERS = 3 * NZ
 WORDS = MEMBERS // 2
 ROWS = WORDS * QUADS
+FIRST_MOVES = 9
 CODES = 32767
 OCTAVES = 28.0
 TOP = 4.0
@@ -112,7 +113,7 @@
 
 def body(
     density, radial_velocity, azimuthal_velocity, shift_far, rest_far, kernel, first, last, twiddle, straight,
-    back, moved_out, potential,
+    back, density_out, radial_out, azimuthal_out, potential,
     ext, sect, coef, weight, row_send, row_in, tile_in, col_send, col_in, move_out, cycle_in, cycle_out,
     move_in, surf_out, surf_in, spec_out, spec_in, modes_out, modes_in, pot_out, pot_in, lines, back_out,
     back_in, kern, t_first, t_last, t_twiddle, t_straight, t_back,
@@ -177,6 +178,13 @@
 
     for load in loads[:3]:
         load.wait()
+    for c in range(3):
+        heights = [ext[NZ * c + z, pl.ds(0, SLAB), pl.ds(0, SEG)] for z in range(NZ)]
+        total = (heights[0] + heights[1]) + (heights[2] + heights[3])
+        for n in range(SLAB):
+            for quad in range(QUADS):
+                surf_out[c, n, quad, :] = total[n, LANES * quad : LANES * (quad + 1)]
+
     lane_tile = iota((SLAB, LANES), 1)
     mixed = []
     for m in range(MEMBERS):
@@ -191,14 +199,49 @@
     col_send[0] = columns[LANES - 8 :]
     col_send[1] = columns[:8]
 
+
+    finish = []
+
+    def to_azi(n, src, dst, step):
+        return pltpu.make_async_remote_copy(
+            src_ref=src, dst_ref=dst, send_sem=send_sem.at[n], recv_sem=recv_sem.at[n],
+            device_id={"rad": rad, "azi": lax.rem(azi + step, AZI)}, device_id_type=MESH,
+        )
+
+    def to_rad(n, src, dst, step):
+        return pltpu.make_async_remote_copy(
+            src_ref=src, dst_ref=dst, send_sem=send_sem.at[n], recv_sem=recv_sem.at[n],
+            device_id={"rad": lax.rem(rad + step, RAD), "azi": azi}, device_id_type=MESH,
+        )
+
+    def every(count, make, begin=1, end=None):
+        def one(step, carry):
+            make(lax.rem(step + count // 2 - 2, count - 1) + 1).start()
+            return carry
+
+        lax.fori_loop(begin, end or count, one, 0)
+
+    def rows(index, size=ROWS):
+        return pl.ds(pl.multiple_of(index * size, 8), size)
+
+    def wait_all(n, ref, sem):
+        pltpu.make_async_copy(ref, ref, sem.at[n]).wait()
+
+    def later(n, ref):
+        finish.append(lambda: wait_all(n, ref, send_sem))
+
+    def target(step):
+        return lax.rem(azi + step, AZI)
+
+    def ring(step):
+        return lax.rem(rad + step, RAD)
+
+    pl.semaphore_wait(barrier, AZI - 1 + RAD - 1 + 4)
+
+    every(AZI, lambda s: to_azi(0, surf_out.at[:, target(s)], surf_in.at[:, azi], s))
+    later(0, surf_in.at[:, pl.ds(1, AZI - 1)])
     for c in range(3):
-        heights = [ext[NZ * c + z, pl.ds(0, SLAB), pl.ds(0, SEG)] for z in range(NZ)]
-        total = (heights[0] + heights[1]) + (heights[2] + heights[3])
-        for n in range(SLAB):
-            for quad in range(QUADS):
-                surf_out[c, n, quad, :] = total[n, LANES * quad : LANES * (quad + 1)]
-
-    pl.semaphore_wait(barrier, AZI - 1 + RAD - 1 + 4)
+        surf_in[c, azi] = surf_out[c, azi]
 
     def halo(n, src, dst, r_to, a_to):
         return pltpu.make_async_remote_copy(
@@ -219,46 +262,7 @@
     ]
     for one in halos:
         one.start()
-    finish = [one.wait_send for one in halos]
-    def to_azi(n, src, dst, step):
-        return pltpu.make_async_remote_copy(
-            src_ref=src, dst_ref=dst, send_sem=send_sem.at[n], recv_sem=recv_sem.at[n],
-            device_id={"rad": rad, "azi": lax.rem(azi + step, AZI)}, device_id_type=MESH,
-        )
-
-    def to_rad(n, src, dst, step):
-        return pltpu.make_async_remote_copy(
-            src_ref=src, dst_ref=dst, send_sem=send_sem.at[n], recv_sem=recv_sem.at[n],
-            device_id={"rad": lax.rem(rad + step, RAD), "azi": azi}, device_id_type=MESH,
-        )
-
-    def every(count, make):
-        def one(step, carry):
-            make(step).start()
-            return carry
-
-        lax.fori_loop(1, count, one, 0)
-
-    def rows(index, size=ROWS):
-        return pl.ds(pl.multiple_of(index * size, 8), size)
-
-    def wait_all(n, ref, sem):
-        pltpu.make_async_copy(ref, ref, sem.at[n]).wait()
-
-    def later(n, ref):
-        finish.append(lambda: wait_all(n, ref, send_sem))
-
-    def target(step):
-        return lax.rem(azi + step, AZI)
-
-    def ring(step):
-        return lax.rem(rad + step, RAD)
-
-    every(AZI, lambda s: to_azi(0, surf_out.at[:, target(s)], surf_in.at[:, azi], s))
-    later(0, surf_in.at[:, pl.ds(1, AZI - 1)])
-    for c in range(3):
-        surf_in[c, azi] = surf_out[c, azi]
-
+    finish += [one.wait_send for one in halos]
     for load in loads[3:6]:
         load.wait()
     wait_all(0, surf_in.at[:, pl.ds(1, AZI - 1)], recv_sem)
@@ -338,8 +342,10 @@
                     at = 8 * ROWS * block + WORDS * quad + 2 * c + z // 2
                     move_out[pl.ds(at, 8, stride=ROWS), :] = words[8 * block : 8 * block + 8]
 
-    every(AZI, lambda s: to_azi(1, move_out.at[rows(target(s))], cycle_in.at[rows(azi)], s))
-    later(1, cycle_in.at[pl.ds(0, ROWS * (AZI - 1))])
+    def send_moves(begin, end):
+        every(AZI, lambda s: to_azi(1, move_out.at[rows(target(s))], cycle_in.at[rows(azi)], s), begin, end)
+
+    send_moves(1, FIRST_MOVES)
     cycle_in[rows(azi), :] = move_out[rows(azi), :]
 
     wait_all(2, spec_in.at[pl.ds(1, AZI - 1)], recv_sem)
@@ -353,29 +359,9 @@
         modes_out[n] = packed
     every(RAD, lambda s: to_rad(4, modes_out.at[ring(s)], modes_in.at[rad], s))
     later(4, modes_in.at[pl.ds(1, RAD - 1)])
+    send_moves(FIRST_MOVES, AZI)
+    later(1, cycle_in.at[pl.ds(0, ROWS * (AZI - 1))])
     modes_in[rad] = modes_out[rad]
-
-    wait_all(1, cycle_in.at[pl.ds(0, ROWS * (AZI - 1))], recv_sem)
-    cycle_in[pl.ds(ROWS * AZI, ROWS), :] = cycle_in[pl.ds(0, ROWS), :]
-    my_shift = shift[azi]
-    turn_rows, turn_lanes = my_shift // LANES, my_shift % LANES
-    lane = iota((ROWS, LANES), 1)
-
-    def rotated(segment):
-        start = lax.rem(QUADS * segment + LANES - 1 - turn_rows + LANES, LANES) * WORDS
-        here = cycle_in[pl.ds(start + WORDS, ROWS), :]
-        before = cycle_in[pl.ds(start, ROWS), :]
-        return pltpu.roll(jnp.where(lane < LANES - turn_lanes, here, before), turn_lanes, 1)
-
-    def rotate_and_send(step, carry):
-        segment = target(step)
-        cycle_out[rows(segment), :] = rotated(segment)
-        to_azi(3, cycle_out.at[rows(segment)], move_in.at[rows(azi)], step).start()
-        return carry
-
-    lax.fori_loop(1, AZI, rotate_and_send, 0)
-    later(3, move_in.at[pl.ds(0, ROWS * (AZI - 1))])
-    move_in[rows(azi), :] = rotated(azi)
 
     shape = (16, NR)
     mode = 256 * rad + 8 * azi + iota(shape, 0) // 2
@@ -436,6 +422,29 @@
     every(RAD, lambda s: to_rad(5, pot_out.at[ring(s) // 4], pot_in.at[rad], s))
     later(5, pot_in.at[pl.ds(1, RAD - 1)])
     pot_in[rad] = pot_out[rad // 4]
+    wait_all(1, cycle_in.at[pl.ds(0, ROWS * (AZI - 1))], recv_sem)
+    cycle_in[pl.ds(ROWS * AZI, ROWS), :] = cycle_in[pl.ds(0, ROWS), :]
+    my_shift = shift[azi]
+    turn_rows, turn_lanes = my_shift // LANES, my_shift % LANES
+    lane = iota((ROWS, LANES), 1)
+
+    def rotated(segment):
+        start = lax.rem(QUADS * segment + LANES - 1 - turn_rows + LANES, LANES) * WORDS
+        here = cycle_in[pl.ds(start + WORDS, ROWS), :]
+        before = cycle_in[pl.ds(start, ROWS), :]
+        return pltpu.roll(jnp.where(lane < LANES - turn_lanes, here, before), turn_lanes, 1)
+
+    def rotate_and_send(step, carry):
+        step = lax.rem(step + AZI // 2 - 2, AZI - 1) + 1
+        segment = target(step)
+        cycle_out[rows(segment), :] = rotated(segment)
+        to_azi(3, cycle_out.at[rows(segment)], move_in.at[rows(azi)], step).start()
+        return carry
+
+    lax.fori_loop(1, AZI, rotate_and_send, 0)
+    later(3, move_in.at[pl.ds(0, ROWS * (AZI - 1))])
+    move_in[rows(azi), :] = rotated(azi)
+
     wait_all(5, pot_in.at[pl.ds(1, RAD - 1)], recv_sem)
     lines[...] = pot_in[...].reshape(LANES, LANES).T
     gathered = lines[rows(lax.rem(rad, 4), SLAB), :]
@@ -444,6 +453,17 @@
     every(AZI, lambda s: to_azi(6, back_out.at[target(s)], back_in.at[azi], s))
     later(6, back_in.at[pl.ds(1, AZI - 1)])
     back_in[azi] = back_out[azi]
+    wait_all(3, move_in.at[pl.ds(0, ROWS * (AZI - 1))], recv_sem)
+    for c, out in enumerate((density_out, radial_out, azimuthal_out)):
+        for pair in range(NZ // 2):
+            for quad in range(QUADS):
+                for block in range(SLAB // 8):
+                    at = 8 * ROWS * block + WORDS * quad + 2 * c + pair
+                    words = move_in[pl.ds(at, 8, stride=ROWS), :]
+                    place = pl.ds(8 * block, 8), pl.ds(LANES * quad, LANES)
+                    out[2 * pair, *place] = decode((words << 16) >> 16)
+                    out[2 * pair + 1, *place] = decode(words >> 16)
+
     for load in loads[7:9]:
         load.wait()
     wait_all(6, back_in.at[pl.ds(1, AZI - 1)], recv_sem)
@@ -459,38 +479,32 @@
     joined = jnp.concatenate([real * turn_cos - imag * turn_sin, real * turn_sin + imag * turn_cos], axis=0)
     potential[...] = dot(t_last[...], joined)
 
-    wait_all(3, move_in.at[pl.ds(0, ROWS * (AZI - 1))], recv_sem)
-    moved_out[...] = move_in[...]
 
     for wait in finish:
         wait()
 
 
-def unpack(move_in, lines, density_out, radial_out, azimuthal_out, potential):
-    for c, out in enumerate((density_out, radial_out, azimuthal_out)):
-        for pair in range(NZ // 2):
-            for quad in range(QUADS):
-                for block in range(SLAB // 8):
-                    at = 8 * ROWS * block + WORDS * quad + 2 * c + pair
-                    words = move_in[pl.ds(at, 8, stride=ROWS), :]
-                    place = pl.ds(8 * block, 8), pl.ds(LANES * quad, LANES)
-                    out[2 * pair, *place] = decode((words << 16) >> 16)
-                    out[2 * pair + 1, *place] = decode(words >> 16)
-    potential[...] = lines[...]
+def unload(*refs):
+    pairs, sems = zip(refs[:4], refs[4:8]), refs[8]
+    copies = [pltpu.make_async_copy(src, dst, sems.at[n]) for n, (src, dst) in enumerate(pairs)]
+    for copy in copies:
+        copy.start()
+    for copy in copies:
+        copy.wait()
 
 
 def step(density, radial_velocity, azimuthal_velocity, cycle_shift, remainder, kernel):
     whole = pl.BlockSpec(memory_space=pltpu.VMEM)
     away = pl.BlockSpec(memory_space=pltpu.HBM)
-    block = jax.ShapeDtypeStruct((NZ, SLAB, SEG), F32)
+    shapes = [jax.ShapeDtypeStruct((NZ, SLAB, SEG), F32)] * 3 + [jax.ShapeDtypeStruct((128, 128), F32)]
     moves = pltpu.VMEM((ROWS * AZI, LANES), jnp.int32)
     single = pltpu.VMEM((AZI, 1, LANES), F32)
-    moved, lines = pl.pallas_call(
+    results = pl.pallas_call(
         body,
         name="disc_step",
-        out_shape=[jax.ShapeDtypeStruct((ROWS * AZI, LANES), jnp.int32), jax.ShapeDtypeStruct((128, 128), F32)],
+        out_shape=shapes,
         in_specs=[away] * 11,
-        out_specs=[whole] * 2,
+        out_specs=[whole] * 4,
         scratch_shapes=[
             pltpu.VMEM((MEMBERS, EXT_R, EXT_P), F32),
             pltpu.VMEM((MEMBERS, EXT_R, EXT_P), F32),
@@ -543,13 +557,14 @@
         ]
     )
     *fields, potential = pl.pallas_call(
-        unpack,
-        name="unpack",
-        out_shape=[block, block, block, jax.ShapeDtypeStruct((128, 128), F32)],
-        in_specs=[whole] * 2,
-        out_specs=[whole] * 4,
+        unload,
+        name="unload",
+        out_shape=shapes,
+        in_specs=[whole] * 4,
+        out_specs=[pl.BlockSpec(memory_space=pl.ANY)] * 4,
+        scratch_shapes=[pltpu.SemaphoreType.DMA((4,))],
         compiler_params=pltpu.CompilerParams(vmem_limit_bytes=8 * 1024 * 1024),
-    )(moved, lines)
+    )(*results)
     return *fields, potential.reshape(1, NPHI)
 
 

time: 47.6 us -> 43.7 us (0.918)
  Pallas kernels: 46.9 us -> 43 us
    pallas_call x2, Pallas kernels: 46.9 us -> 43 us  [the longest x1 42 us: step(): pl.pallas_call(body, name='disc_step', out_shape=shapes, in_specs=[away]...]
where the time goes in v3:
time: 43.7 us; the launch traced here: 43.6 us
  Pallas kernels  43 us (98%)
  between operations  0.64 us (1%)
    pallas_call x1, Pallas kernels, step(): pl.pallas_call(body, name='disc_step', out_shape=shapes, in_specs=[away]...  42 us
    pallas_call x1, Pallas kernels, step(): pl.pallas_call(unload, name='unload', out_shape=shapes, in_specs=[whole]...  0.93 us

profile of v3, /device:TPU:1, one launch (start us, length us, event | category | flops | bytes accessed | tf_op | source)
XLA Modules:
  0.0 43.6 jit_solution(13749629941982657788)
XLA Ops:
  0.6 42.0 %disc_step.1 = (f32[4,32,512]{2,1,0:T(8,128)S(1)}, f32[4,32,512]{2,1,0:T(8,128)S(1)}, f32[4,32,512]{2,1,0:T(8,128)S(1)}, f32[128,128]{1,0:T(8,128)S(1)}) custom-call(f32[4,32,512]{2,1,0:T(8,128)} %density.1, f32[4,32,512]{2,1,0:T(8,128)} %radial_velocity.1, f32[4,32,512]{2,1,0:T(8,128)} %azimuthal_velocity.1, s32[32]{0:T(128)} %shift_far.1, f32[32]{0:T(128)} %rest_far.1, ...), custom_call_target="tpu_custom_call" | custom-call | tf_op jit(solution)/shard_map/disc_step/pallas_call | solution.py:502
  42.7 0.9 %unload.1 = (f32[4,32,512]{2,1,0:T(8,128)}, f32[4,32,512]{2,1,0:T(8,128)}, f32[4,32,512]{2,1,0:T(8,128)}, f32[128,128]{1,0:T(8,128)}) custom-call(f32[4,32,512]{2,1,0:T(8,128)S(1)} %get-tuple-element.12.refs_0_, f32[4,32,512]{2,1,0:T(8,128)S(1)} %get-tuple-element.13.refs_1_, f32[4,32,512]{2,1,0:T(8,128)S(1)} %get-tuple-element.14.refs_2_, ...), custom_call_target="tpu_custom_call" | custom-call | tf_op jit(solution)/shard_map/unload/pallas_call | solution.py:559

commit v4 on v3

--- a/solution.py
+++ b/solution.py
@@ -50,11 +50,27 @@
     back = np.concatenate(
         [np.where(real, cos.T, -sin.T), np.where(real, sin.T, cos.T)], axis=1
     )
-    return [t.astype(np.float32) for t in (first, last, twiddle, straight, back)]
+    pairs = []
+    for table in (last, back):
+        high = table.astype(jnp.bfloat16)
+        pairs.append(np.stack([high, (table - high.astype(np.float64)).astype(jnp.bfloat16)]))
+    return [t.astype(np.float32) for t in (first, twiddle, straight)] + pairs
 
 
 def dot(left, right):
     return jnp.dot(left, right, precision=HIGHEST, preferred_element_type=F32)
+
+
+def halves_of(value):
+    high = value.astype(jnp.bfloat16)
+    return high, (value - high.astype(F32)).astype(jnp.bfloat16)
+
+
+def dot_split(left, right):
+    def part(a, b):
+        return jnp.dot(a, b, preferred_element_type=F32)
+
+    return part(left[0], right[0]) + (part(left[0], right[1]) + part(left[1], right[0]))
 
 
 def iota(shape, axis):
@@ -112,7 +128,7 @@
 
 
 def body(
-    density, radial_velocity, azimuthal_velocity, shift_far, rest_far, kernel, first, last, twiddle, straight,
+    density, radial_velocity, azimuthal_velocity, shift_far, rest_far, kernel, first, twiddle, straight, last,
     back, density_out, radial_out, azimuthal_out, potential,
     ext, sect, coef, weight, row_send, row_in, tile_in, col_send, col_in, move_out, cycle_in, cycle_out,
     move_in, surf_out, surf_in, spec_out, spec_in, modes_out, modes_in, pot_out, pot_in, lines, back_out,
@@ -469,15 +485,16 @@
     wait_all(6, back_in.at[pl.ds(1, AZI - 1)], recv_sem)
     values = back_in[:, 0, :]
     values = jnp.concatenate([values[:16], values[16:]], axis=1)
-    spread = (iota((128, 16), 0) // 8 == iota((128, 16), 1)).astype(F32)
+    spread = (iota((128, 16), 0) // 8 == iota((128, 16), 1)).astype(F32).astype(jnp.bfloat16)
+    high, low = [jnp.dot(spread, piece, preferred_element_type=F32) for piece in halves_of(values)]
     zero_mode = (iota((128, 256), 0) == 0) & (iota((128, 256), 1) < 2)
     own = iota((128, 256), 0) % 8 == iota((128, 256), 1) // 2 % 8
-    values = jnp.where(own, dot(spread, values) * jnp.where(zero_mode, 1.0 / NPHI, 2.0 / NPHI), 0.0)
-    pieces = dot(values, t_back[...])
+    values = jnp.where(own, (high + low) * jnp.where(zero_mode, 1.0 / NPHI, 2.0 / NPHI), 0.0)
+    pieces = dot_split(halves_of(values), (t_back[0], t_back[1]))
     real, imag = pieces[:, :128], pieces[:, 128:]
     turn_cos, turn_sin = t_twiddle[:128], t_twiddle[128:]
     joined = jnp.concatenate([real * turn_cos - imag * turn_sin, real * turn_sin + imag * turn_cos], axis=0)
-    potential[...] = dot(t_last[...], joined)
+    potential[...] = dot_split((t_last[0], t_last[1]), halves_of(joined))
 
 
     for wait in finish:
@@ -532,10 +549,10 @@
             single,
             pltpu.VMEM((8, NR, NR), jnp.bfloat16),
             pltpu.VMEM((256, 128), F32),
-            pltpu.VMEM((128, 256), F32),
+            pltpu.VMEM((2, 128, 256), jnp.bfloat16),
             pltpu.VMEM((256, 128), F32),
             pltpu.VMEM((256, 256), F32),
-            pltpu.VMEM((256, 256), F32),
+            pltpu.VMEM((2, 256, 256), jnp.bfloat16),
             pltpu.SMEM((SLAB,), jnp.int32),
             pltpu.SMEM((SLAB,), F32),
             pltpu.SemaphoreType.DMA((11,)),

time: 43.7 us -> 43.4 us (level)
  no operation moved by 1% of the time
where the time goes in v4:
time: 43.4 us; the launch traced here: 43.3 us
  Pallas kernels  42.7 us (98%)
  between operations  0.64 us (1%)
    pallas_call x1, Pallas kernels, step(): pl.pallas_call(body, name='disc_step', out_shape=shapes, in_specs=[away]...  41.7 us
    pallas_call x1, Pallas kernels, step(): pl.pallas_call(unload, name='unload', out_shape=shapes, in_specs=[whole]...  0.93 us

profile of v4, /device:TPU:1, one launch (start us, length us, event | category | flops | bytes accessed | tf_op | source)
XLA Modules:
  0.0 43.3 jit_solution(2961246432440082126)
XLA Ops:
  0.6 41.7 %disc_step.1 = (f32[4,32,512]{2,1,0:T(8,128)S(1)}, f32[4,32,512]{2,1,0:T(8,128)S(1)}, f32[4,32,512]{2,1,0:T(8,128)S(1)}, f32[128,128]{1,0:T(8,128)S(1)}) custom-call(f32[4,32,512]{2,1,0:T(8,128)} %density.1, f32[4,32,512]{2,1,0:T(8,128)} %radial_velocity.1, f32[4,32,512]{2,1,0:T(8,128)} %azimuthal_velocity.1, s32[32]{0:T(128)} %shift_far.1, f32[32]{0:T(128)} %rest_far.1, ...), custom_call_target="tpu_custom_call" | custom-call | tf_op jit(solution)/shard_map/disc_step/pallas_call | solution.py:519
  42.4 0.9 %unload.1 = (f32[4,32,512]{2,1,0:T(8,128)}, f32[4,32,512]{2,1,0:T(8,128)}, f32[4,32,512]{2,1,0:T(8,128)}, f32[128,128]{1,0:T(8,128)}) custom-call(f32[4,32,512]{2,1,0:T(8,128)S(1)} %get-tuple-element.12.refs_0_, f32[4,32,512]{2,1,0:T(8,128)S(1)} %get-tuple-element.13.refs_1_, f32[4,32,512]{2,1,0:T(8,128)S(1)} %get-tuple-element.14.refs_2_, ...), custom_call_target="tpu_custom_call" | custom-call | tf_op jit(solution)/shard_map/unload/pallas_call | solution.py:576

commit v5 on v4

--- a/solution.py
+++ b/solution.py
@@ -174,6 +174,94 @@
     lax.fori_loop(1, AZI, greet_azi, 0)
     lax.fori_loop(1, RAD, greet_rad, 0)
 
+    for load in loads[:3]:
+        load.wait()
+    for c in range(3):
+        heights = [ext[NZ * c + z, pl.ds(0, SLAB), pl.ds(0, SEG)] for z in range(NZ)]
+        total = (heights[0] + heights[1]) + (heights[2] + heights[3])
+        for n in range(SLAB):
+            for quad in range(QUADS):
+                surf_out[c, n, quad, :] = total[n, LANES * quad : LANES * (quad + 1)]
+
+    lane_tile = iota((SLAB, LANES), 1)
+    mixed = []
+    for m in range(MEMBERS):
+        low = ext[m, pl.ds(0, SLAB), pl.ds(0, LANES)]
+        high = ext[m, pl.ds(0, SLAB), pl.ds(SEG - LANES, LANES)]
+        edge = jnp.where(lane_tile < LANES // 2, low, high)
+        mixed.append(edge)
+        for n, at in enumerate((SLAB - 2, 0)):
+            row_send[n, pl.ds(2 * m, 2), pl.ds(0, SEG)] = ext[m, pl.ds(at, 2), pl.ds(0, SEG)]
+            row_send[n, pl.ds(2 * m, 2), pl.ds(SEG, LANES)] = edge[at : at + 2]
+    columns = jnp.concatenate(mixed, axis=0).T
+    col_send[0] = columns[LANES - 8 :]
+    col_send[1] = columns[:8]
+
+
+    finish = []
+
+    def to_azi(n, src, dst, step):
+        return pltpu.make_async_remote_copy(
+            src_ref=src, dst_ref=dst, send_sem=send_sem.at[n], recv_sem=recv_sem.at[n],
+            device_id={"rad": rad, "azi": lax.rem(azi + step, AZI)}, device_id_type=MESH,
+        )
+
+    def to_rad(n, src, dst, step):
+        return pltpu.make_async_remote_copy(
+            src_ref=src, dst_ref=dst, send_sem=send_sem.at[n], recv_sem=recv_sem.at[n],
+            device_id={"rad": lax.rem(rad + step, RAD), "azi": azi}, device_id_type=MESH,
+        )
+
+    def every(count, make, begin=1, end=None):
+        def one(step, carry):
+            make(lax.rem(step + count // 2 - 2, count - 1) + 1).start()
+            return carry
+
+        lax.fori_loop(begin, end or count, one, 0)
+
+    def rows(index, size=ROWS):
+        return pl.ds(pl.multiple_of(index * size, 8), size)
+
+    def wait_all(n, ref, sem):
+        pltpu.make_async_copy(ref, ref, sem.at[n]).wait()
+
+    def later(n, ref):
+        finish.append(lambda: wait_all(n, ref, send_sem))
+
+    def target(step):
+        return lax.rem(azi + step, AZI)
+
+    def ring(step):
+        return lax.rem(rad + step, RAD)
+
+    pl.semaphore_wait(barrier, AZI - 1 + RAD - 1 + 4)
+
+    every(AZI, lambda s: to_azi(0, surf_out.at[:, target(s)], surf_in.at[:, azi], s))
+    later(0, surf_in.at[:, pl.ds(1, AZI - 1)])
+    for c in range(3):
+        surf_in[c, azi] = surf_out[c, azi]
+
+    def halo(n, src, dst, r_to, a_to):
+        return pltpu.make_async_remote_copy(
+            src_ref=src, dst_ref=dst, send_sem=halo_send.at[n], recv_sem=halo_recv.at[n],
+            device_id={"rad": r_to, "azi": a_to}, device_id_type=MESH,
+        )
+
+    plain, corner = pl.ds(0, SEG), pl.ds(SEG, LANES)
+    halos = [
+        halo(0, row_send.at[0, :, plain], row_in.at[0], outer, azi),
+        halo(1, row_send.at[1, :, plain], row_in.at[1], inner, azi),
+        halo(2, col_send.at[0], col_in.at[pl.ds(LANES - 8, 8)], rad, right),
+        halo(3, col_send.at[1], col_in.at[pl.ds(0, 8)], rad, left),
+        halo(4, row_send.at[0, :, corner], tile_in.at[0], outer, right),
+        halo(5, row_send.at[0, :, corner], tile_in.at[1], outer, left),
+        halo(6, row_send.at[1, :, corner], tile_in.at[2], inner, right),
+        halo(7, row_send.at[1, :, corner], tile_in.at[3], inner, left),
+    ]
+    for one in halos:
+        one.start()
+    finish += [one.wait_send for one in halos]
+
     row = iota((EXT_R, LANES), 0)
     cycle = SLAB * rad + jnp.where(row < SLAB + 4, row, row - EXT_R)
     radius = 1.0 + 4.0 * (cycle.astype(F32) + 0.5) / NR
@@ -192,93 +280,6 @@
             weight[n, pl.ds(8 * block, 8), :] = value
     ext[:, pl.ds(SLAB, 8), :] = jnp.zeros((MEMBERS, 8, EXT_P), F32)
 
-    for load in loads[:3]:
-        load.wait()
-    for c in range(3):
-        heights = [ext[NZ * c + z, pl.ds(0, SLAB), pl.ds(0, SEG)] for z in range(NZ)]
-        total = (heights[0] + heights[1]) + (heights[2] + heights[3])
-        for n in range(SLAB):
-            for quad in range(QUADS):
-                surf_out[c, n, quad, :] = total[n, LANES * quad : LANES * (quad + 1)]
-
-    lane_tile = iota((SLAB, LANES), 1)
-    mixed = []
-    for m in range(MEMBERS):
-        low = ext[m, pl.ds(0, SLAB), pl.ds(0, LANES)]
-        high = ext[m, pl.ds(0, SLAB), pl.ds(SEG - LANES, LANES)]
-        edge = jnp.where(lane_tile < LANES // 2, low, high)
-        mixed.append(edge)
-        for n, at in enumerate((SLAB - 2, 0)):
-            row_send[n, pl.ds(2 * m, 2), pl.ds(0, SEG)] = ext[m, pl.ds(at, 2), pl.ds(0, SEG)]
-            row_send[n, pl.ds(2 * m, 2), pl.ds(SEG, LANES)] = edge[at : at + 2]
-    columns = jnp.concatenate(mixed, axis=0).T
-    col_send[0] = columns[LANES - 8 :]
-    col_send[1] = columns[:8]
-
-
-    finish = []
-
-    def to_azi(n, src, dst, step):
-        return pltpu.make_async_remote_copy(
-            src_ref=src, dst_ref=dst, send_sem=send_sem.at[n], recv_sem=recv_sem.at[n],
-            device_id={"rad": rad, "azi": lax.rem(azi + step, AZI)}, device_id_type=MESH,
-        )
-
-    def to_rad(n, src, dst, step):
-        return pltpu.make_async_remote_copy(
-            src_ref=src, dst_ref=dst, send_sem=send_sem.at[n], recv_sem=recv_sem.at[n],
-            device_id={"rad": lax.rem(rad + step, RAD), "azi": azi}, device_id_type=MESH,
-        )
-
-    def every(count, make, begin=1, end=None):
-        def one(step, carry):
-            make(lax.rem(step + count // 2 - 2, count - 1) + 1).start()
-            return carry
-
-        lax.fori_loop(begin, end or count, one, 0)
-
-    def rows(index, size=ROWS):
-        return pl.ds(pl.multiple_of(index * size, 8), size)
-
-    def wait_all(n, ref, sem):
-        pltpu.make_async_copy(ref, ref, sem.at[n]).wait()
-
-    def later(n, ref):
-        finish.append(lambda: wait_all(n, ref, send_sem))
-
-    def target(step):
-        return lax.rem(azi + step, AZI)
-
-    def ring(step):
-        return lax.rem(rad + step, RAD)
-
-    pl.semaphore_wait(barrier, AZI - 1 + RAD - 1 + 4)
-
-    every(AZI, lambda s: to_azi(0, surf_out.at[:, target(s)], surf_in.at[:, azi], s))
-    later(0, surf_in.at[:, pl.ds(1, AZI - 1)])
-    for c in range(3):
-        surf_in[c, azi] = surf_out[c, azi]
-
-    def halo(n, src, dst, r_to, a_to):
-        return pltpu.make_async_remote_copy(
-            src_ref=src, dst_ref=dst, send_sem=halo_send.at[n], recv_sem=halo_recv.at[n],
-            device_id={"rad": r_to, "azi": a_to}, device_id_type=MESH,
-        )
-
-    plain, corner = pl.ds(0, SEG), pl.ds(SEG, LANES)
-    halos = [
-        halo(0, row_send.at[0, :, plain], row_in.at[0], outer, azi),
-        halo(1, row_send.at[1, :, plain], row_in.at[1], inner, azi),
-        halo(2, col_send.at[0], col_in.at[pl.ds(LANES - 8, 8)], rad, right),
-        halo(3, col_send.at[1], col_in.at[pl.ds(0, 8)], rad, left),
-        halo(4, row_send.at[0, :, corner], tile_in.at[0], outer, right),
-        halo(5, row_send.at[0, :, corner], tile_in.at[1], outer, left),
-        halo(6, row_send.at[1, :, corner], tile_in.at[2], inner, right),
-        halo(7, row_send.at[1, :, corner], tile_in.at[3], inner, left),
-    ]
-    for one in halos:
-        one.start()
-    finish += [one.wait_send for one in halos]
     for load in loads[3:6]:
         load.wait()
     wait_all(0, surf_in.at[:, pl.ds(1, AZI - 1)], recv_sem)

time: 43.4 us -> 43.4 us (level)
  no operation moved by 1% of the time
where the time goes in v5:
time: 43.4 us; the launch traced here: 43.3 us
  Pallas kernels  42.7 us (98%)
  between operations  0.64 us (1%)
    pallas_call x1, Pallas kernels, step(): pl.pallas_call(body, name='disc_step', out_shape=shapes, in_specs=[away]...  41.7 us
    pallas_call x1, Pallas kernels, step(): pl.pallas_call(unload, name='unload', out_shape=shapes, in_specs=[whole]...  0.93 us

profile of v5, /device:TPU:1, one launch (start us, length us, event | category | flops | bytes accessed | tf_op | source)
XLA Modules:
  0.0 43.3 jit_solution(5897745511374835411)
XLA Ops:
  0.6 41.7 %disc_step.1 = (f32[4,32,512]{2,1,0:T(8,128)S(1)}, f32[4,32,512]{2,1,0:T(8,128)S(1)}, f32[4,32,512]{2,1,0:T(8,128)S(1)}, f32[128,128]{1,0:T(8,128)S(1)}) custom-call(f32[4,32,512]{2,1,0:T(8,128)} %density.1, f32[4,32,512]{2,1,0:T(8,128)} %radial_velocity.1, f32[4,32,512]{2,1,0:T(8,128)} %azimuthal_velocity.1, s32[32]{0:T(128)} %shift_far.1, f32[32]{0:T(128)} %rest_far.1, ...), custom_call_target="tpu_custom_call" | custom-call | tf_op jit(solution)/shard_map/disc_step/pallas_call | solution.py:520
  42.4 0.9 %unload.1 = (f32[4,32,512]{2,1,0:T(8,128)}, f32[4,32,512]{2,1,0:T(8,128)}, f32[4,32,512]{2,1,0:T(8,128)}, f32[128,128]{1,0:T(8,128)}) custom-call(f32[4,32,512]{2,1,0:T(8,128)S(1)} %get-tuple-element.12.refs_0_, f32[4,32,512]{2,1,0:T(8,128)S(1)} %get-tuple-element.13.refs_1_, f32[4,32,512]{2,1,0:T(8,128)S(1)} %get-tuple-element.14.refs_2_, ...), custom_call_target="tpu_custom_call" | custom-call | tf_op jit(solution)/shard_map/unload/pallas_call | solution.py:577
